TPU v7x, 512 devices: a whole 4x4x16 slice. The times are simulated.
512 devices in a mesh: ch: 32 (over z, core), lat: 4 (over y), lon: 4 (over x).
Axes of the slice: x: 4, y: 4, z: 16, core: 2. Of those that a mesh axis runs over, the one named last changes fastest.
Arguments:
- inputs: bfloat16 [512, 4, 16, 192], P('ch', None, 'lat', 'lon'), may hold values from -6 to 6
- weights: bfloat16 [512, 27, 512], P('ch'), may hold values from -0.0546875 to 0.0546875
- out_grad: bfloat16 [512, 4, 16, 192], P('ch', None, 'lat', 'lon'), may hold values from -6 to 6
Outputs:
- input_grad: bfloat16 [512, 4, 16, 192], P('ch', None, 'lat', 'lon')
- weight_grad: float32 [512, 27, 512], P('ch')
All inputs are finite; a program needn't handle non-finite values.
Results may differ from a plain program's by a relative error of at most 0.001.
Values may be sent and summed in bfloat16 or wider, within the bound.
A program may use at most 64 MiB of HBM per device.

v0:
```python
import math

import jax
import jax.numpy as jnp
from jax import lax
from jax.sharding import PartitionSpec as P


def padded_2(cells, sides, width):
    for axis, dim in sides:
        count = lax.axis_size(axis)
        head = lax.slice_in_dim(cells, 0, width, axis=dim)
        tail = lax.slice_in_dim(cells, cells.shape[dim] - width, cells.shape[dim], axis=dim)
        cells = jnp.concatenate(
            [
                lax.ppermute(tail, axis, [(i, (i + 1) % count) for i in range(count)]),
                cells,
                lax.ppermute(head, axis, [((i + 1) % count, i) for i in range(count)]),
            ],
            axis=dim,
        )
    return cells


def mask_rims(padded):
    count = lax.axis_size("lat")
    where_lat = lax.axis_index("lat")
    lines = jnp.arange(padded.shape[2])
    drop = (lines == 0) & (where_lat == 0) | (lines == padded.shape[2] - 1) & (
        where_lat == count - 1
    )
    return jnp.where(drop[None, None, :, None], jnp.zeros((), padded.dtype), padded)


def pad_levels(field):
    return jnp.pad(field, ((0, 0), (1, 1), (0, 0), (0, 0)))


def body(inputs, weights, out_grad):
    chans, levels, height, width = inputs.shape
    input_pad = pad_levels(mask_rims(padded_2(inputs, (("lat", 2), ("lon", 3)), 1)))
    grad_inner = lax.all_gather(out_grad, "ch", axis=0, tiled=True)
    grad_pad = pad_levels(mask_rims(padded_2(grad_inner, (("lat", 2), ("lon", 3)), 1)))
    filters = grad_pad.shape[0]
    products = jnp.dot(
        weights.reshape(chans * 27, filters),
        grad_pad.reshape(filters, -1),
        preferred_element_type=jnp.float32,
    )
    products = products.reshape((chans, 27) + tuple(grad_pad.shape[1:]))
    total = jnp.zeros((chans, levels, height, width), jnp.float32)
    pieces = []
    for tap in range(27):
        shift_lev = tap // 9 - 1
        shift_lat = tap // 3 % 3 - 1
        shift_lon = tap % 3 - 1
        total = (
            total
            + products[
                :,
                tap,
                1 - shift_lev : 1 - shift_lev + levels,
                1 - shift_lat : 1 - shift_lat + height,
                1 - shift_lon : 1 - shift_lon + width,
            ]
        )
        pieces.append(
            input_pad[
                :,
                1 + shift_lev : 1 + shift_lev + levels,
                1 + shift_lat : 1 + shift_lat + height,
                1 + shift_lon : 1 + shift_lon + width,
            ]
        )
    columns = jnp.stack(pieces, axis=1).reshape(chans * 27, -1)
    partial_grad = lax.dot_general(
        columns,
        grad_inner.reshape(filters, -1),
        (((1,), (1,)), ((), ())),
        preferred_element_type=jnp.float32,
    )
    summed = lax.psum(partial_grad, ("lat", "lon"))
    cells = levels * height * width * lax.axis_size("lat") * lax.axis_size("lon")
    weight_grad = (summed * (1.0 / math.sqrt(cells))).reshape(chans, 27, filters)
    return (total.astype(jnp.bfloat16), weight_grad)


def solution(mesh):
    in_specs = (P("ch", None, "lat", "lon"), P("ch", None, None), P("ch", None, "lat", "lon"))
    out_specs = (P("ch", None, "lat", "lon"), P("ch", None, None))
    return jax.shard_map(body, mesh=mesh, in_specs=in_specs, out_specs=out_specs, check_vma=False)
```

profile of v0, /device:TPU:1, one launch (start us, length us, event | category | flops | bytes accessed | tf_op | source)
XLA Modules:
  0.0 247.2 jit_solution(15607864098014346800)
XLA Ops:
  8.2 4.0 %collective-permute-start.4 = (bf16[16,4,1,48]{3,2,1,0:T(2,128)(2,1)S(1)}, bf16[16,4,1,48]{3,2,1,0:T(2,128)(2,1)S(1)}, u32[]{:S(2)}, u32[]{:S(2)}) collective-permute-start(bf16[16,4,1,48]{3,2,1,0:T(2,128)(2,1)S(1)} %get-tuple-element.18), channel_id=1, source_target_pairs={{0,4},{4,8},{8,12},{12,0},{1,5},{5,9},{9,13},{13,1},{2,6},{6,10},{... | collective-permute-start | bytes 18440 | tf_op jit(solution)/shard_map/ppermute | solution.py:16
  12.2 3.4 %collective-permute-start.5 = (bf16[16,4,1,48]{3,2,1,0:T(2,128)(2,1)S(1)}, bf16[16,4,1,48]{3,2,1,0:T(2,128)(2,1)S(1)}, u32[]{:S(2)}, u32[]{:S(2)}) collective-permute-start(bf16[16,4,1,48]{3,2,1,0:T(2,128)(2,1)S(1)} %get-tuple-element.19), channel_id=1, source_target_pairs={{4,0},{8,4},{12,8},{0,12},{5,1},{9,5},{13,9},{1,13},{6,2},{10,6},{... | collective-permute-start | bytes 18440 | tf_op jit(solution)/shard_map/ppermute | solution.py:18
  15.6 43.6 %all_gather.3 = bf16[512,4,4,48]{3,2,1,0:T(4,128)(2,1)S(1)} all-gather(bf16[16,4,4,48]{3,2,1,0:T(4,128)(2,1)} %param.5), channel_id=1, replica_groups=mesh['ch'=32,'lat'=4,'lon'=4] {'ch'}, dimensions={0}, use_global_device_ids=true | all-gather | bytes 811008 | tf_op jit(solution)/shard_map/all_gather | solution.py:42
  59.2 2.3 fusion.74
  61.5 2.3 copy.131
  65.8 2.1 copy.132
  67.9 4.5 %collective-permute-start.1 = (bf16[512,4,1,48]{0,3,2,1:T(8,128)(2,1)}, bf16[512,4,1,48]{0,3,2,1:T(8,128)(2,1)}, u32[]{:S(2)}, u32[]{:S(2)}) collective-permute-start(bf16[512,4,1,48]{0,3,2,1:T(8,128)(2,1)} %copy.132), channel_id=1, source_target_pairs={{4,0},{8,4},{12,8},{0,12},{5,1},{9,5},{13,9},{1,13},{6,2},{10,6},{... | collective-permute-start | bytes 589832 | tf_op jit(solution)/shard_map/ppermute | solution.py:18
  73.4 3.1 %collective-permute-start.6 = (bf16[16,4,6,1]{3,2,1,0:T(8,128)(2,1)}, bf16[16,4,6,1]{3,2,1,0:T(8,128)(2,1)S(1)}, u32[]{:S(2)}, u32[]{:S(2)}) collective-permute-start(bf16[16,4,6,1]{3,2,1,0:T(8,128)(2,1)} %get-tuple-element.16), channel_id=1, source_target_pairs={{0,1},{1,2},{2,3},{3,0},{4,5},{5,6},{6,7},{7,4},{8,9},{9,10},{10,1... | collective-permute-start | bytes 2312 | tf_op jit(solution)/shard_map/ppermute | solution.py:16
  76.6 3.6 %collective-permute-start.7 = (bf16[16,4,6,1]{3,2,1,0:T(8,128)(2,1)}, bf16[16,4,6,1]{3,2,1,0:T(8,128)(2,1)}, u32[]{:S(2)}, u32[]{:S(2)}) collective-permute-start(bf16[16,4,6,1]{3,2,1,0:T(8,128)(2,1)} %get-tuple-element.17), channel_id=1, source_target_pairs={{1,0},{2,1},{3,2},{0,3},{5,4},{6,5},{7,6},{4,7},{9,8},{10,9},{11,1... | collective-permute-start | bytes 2312 | tf_op jit(solution)/shard_map/ppermute | solution.py:18
  80.2 2.7 %copy.167 = bf16[512,4,4,48]{0,3,2,1:T(8,128)(2,1)} copy(bf16[512,4,4,48]{3,2,1,0:T(4,128)(2,1)S(1)} %all_gather.3) | data formatting | bytes 1572864 | tf_op jit(solution)/shard_map/all_gather | solution.py:42
  90.0 4.8 %reshape.38 = bf16[432,768]{1,0:T(8,128)(2,1)} reshape(bf16[16,27,4,4,48]{4,3,2,1,0:T(4,128)(2,1)} %copy.166) | data formatting | bytes 1327104 | tf_op jit(solution)/shard_map/reshape | solution.py:75
  94.8 2.1 copy.133
  96.9 3.3 %copy.134 = bf16[512,4,1,48]{3,2,1,0:T(2,128)(2,1)} copy(bf16[512,4,1,48]{0,3,2,1:T(8,128)(2,1)} %collective-permute-done.1) | data formatting | bytes 393216 | tf_op jit(solution)/shard_map/ppermute | solution.py:18
  100.3 5.4 %pad_maximum_fusion = bf16[512,4,6,48]{3,2,1,0:T(8,128)(2,1)S(1)} fusion(bf16[512,4,1,48]{3,2,1,0:T(2,128)(2,1)} %copy.134, bf16[512,4,4,48]{3,2,1,0:T(4,128)(2,1)S(1)} %all_gather.3, bf16[512,4,1,48]{3,2,1,0:T(2,128)(2,1)S(1)} %copy.133), kind=kLoop, calls=%fused_computation | loop fusion | flops 3538944 | bytes 2359296 | tf_op jit(solution)/shard_map/concatenate | solution.py:14
  105.7 4.5 %fusion.73 = (bf16[512,4,6,1]{3,2,1,0:T(8,128)(2,1)}, bf16[512,4,6,1]{3,2,1,0:T(8,128)(2,1)}) fusion(bf16[512,4,6,48]{3,2,1,0:T(8,128)(2,1)S(1)} %pad_maximum_fusion), kind=kLoop, calls=%fused_computation.134 | loop fusion | bytes 98304 | tf_op jit(solution)/shard_map/slice | solution.py:13
  110.2 5.4 %copy.135 = bf16[512,4,6,1]{0,1,3,2:T(4,128)(2,1)S(1)} copy(bf16[512,4,6,1]{3,2,1,0:T(8,128)(2,1)} %get-tuple-element.12) | data formatting | bytes 49152 | tf_op jit(solution)/shard_map/slice | solution.py:13
  117.6 5.5 %copy.136 = bf16[512,4,6,1]{0,1,3,2:T(4,128)(2,1)S(1)} copy(bf16[512,4,6,1]{3,2,1,0:T(8,128)(2,1)} %get-tuple-element.13) | data formatting | bytes 49152 | tf_op jit(solution)/shard_map/slice | solution.py:12
  123.1 4.8 %collective-permute-start.3 = (bf16[512,4,6,1]{0,1,3,2:T(4,128)(2,1)S(1)}, bf16[512,4,6,1]{0,1,3,2:T(4,128)(2,1)S(1)}, u32[]{:S(2)}, u32[]{:S(2)}) collective-permute-start(bf16[512,4,6,1]{0,1,3,2:T(4,128)(2,1)S(1)} %copy.136), channel_id=1, source_target_pairs={{1,0},{2,1},{3,2},{0,3},{5,4},{6,5},{7,6},{4,7},{9,8},{10,9},{11,1... | collective-permute-start | bytes 73736 | tf_op jit(solution)/shard_map/ppermute | solution.py:18
  129.4 5.7 %copy.137 = bf16[512,4,6,48]{0,1,3,2:T(4,128)(2,1)S(1)} copy(bf16[512,4,6,48]{3,2,1,0:T(8,128)(2,1)} %copy-done) | data formatting | bytes 2359296 | tf_op jit(solution)/shard_map/concatenate | solution.py:14
  137.9 2.6 %reshape.35 = bf16[512,1800]{0,1:T(8,128)(2,1)S(1)} reshape(bf16[512,6,6,50]{0,3,2,1:T(8,128)(2,1)} %pad.8.clone) | data formatting | bytes 3686400 | tf_op jit(solution)/shard_map/reshape | solution.py:47
  140.5 2.9 %convolution_bitcast_fusion = f32[432,1800]{1,0:T(8,128)} fusion(bf16[512,1800]{0,1:T(8,128)(2,1)S(1)} %reshape.35, bf16[432,512]{1,0:T(8,128)(2,1)S(1)} %copy-done.3), kind=kOutput, calls=%fused_computation.1 | convolution fusion | flops 796262400 | bytes 5395968 | tf_op jit(solution)/shard_map/dot_general | solution.py:45
  143.4 9.5 %reshape.37 = f32[16,27,6,6,50]{4,3,2,1,0:T(8,128)} reshape(f32[432,1800]{1,0:T(8,128)} %convolution_bitcast_fusion) | data formatting | bytes 6220800 | tf_op jit(solution)/shard_map/reshape | solution.py:50
  152.9 5.0 %fusion.1 = bf16[16,4,4,48]{3,2,1,0:T(4,128)(2,1)} fusion(f32[16,27,6,6,50]{4,3,2,1,0:T(8,128)} %reshape.37), kind=kLoop, calls=%fused_computation.24 | loop fusion | flops 331776 | bytes 1351680 | tf_op jit(solution)/shard_map/convert_element_type | solution.py:85
  157.9 79.7 %all-reduce.4.cloned.1.call-done = f32[432,512]{1,0:T(8,128)} async-done(((f32[432,512]{1,0:T(8,128)}), f32[432,512]{1,0:T(8,128)}) %all-reduce.4.cloned.1.call-update) | async-done | bytes 884752 | tf_op jit(solution)/shard_map/psum | solution.py:82
  (74 shorter events, 19.9 us)
Async XLA Ops:
  7.2 230.4 %all-reduce.4.cloned.1.call-start = ((), (), s32[]{:S(2)}) async-start(), calls=%async_computation | async-start | bytes 1769472 | tf_op jit(solution)/shard_map/psum | solution.py:82
  8.2 64.3 %collective-permute-start.4 = (bf16[16,4,1,48]{3,2,1,0:T(2,128)(2,1)S(1)}, bf16[16,4,1,48]{3,2,1,0:T(2,128)(2,1)S(1)}, u32[]{:S(2)}, u32[]{:S(2)}) collective-permute-start(bf16[16,4,1,48]{3,2,1,0:T(2,128)(2,1)S(1)} %get-tuple-element.18), channel_id=1, source_target_pairs={{0,4},{4,8},{8,12},{12,0},{1,5},{5,9},{9,13},{13,1},{2,6},{6,10},{... | collective-permute-start | bytes 18440 | tf_op jit(solution)/shard_map/ppermute | solution.py:16
  12.2 60.2 %collective-permute-start.5 = (bf16[16,4,1,48]{3,2,1,0:T(2,128)(2,1)S(1)}, bf16[16,4,1,48]{3,2,1,0:T(2,128)(2,1)S(1)}, u32[]{:S(2)}, u32[]{:S(2)}) collective-permute-start(bf16[16,4,1,48]{3,2,1,0:T(2,128)(2,1)S(1)} %get-tuple-element.19), channel_id=1, source_target_pairs={{4,0},{8,4},{12,8},{0,12},{5,1},{9,5},{13,9},{1,13},{6,2},{10,6},{... | collective-permute-start | bytes 18440 | tf_op jit(solution)/shard_map/ppermute | solution.py:18
  61.5 11.0 %copy-start.4 = (bf16[16,4,4,48]{3,2,1,0:T(4,128)(2,1)S(1)}, bf16[16,4,4,48]{3,2,1,0:T(4,128)(2,1)}, u32[]{:S(2)}) copy-start(bf16[16,4,4,48]{3,2,1,0:T(4,128)(2,1)} %param.3) | copy-start | bytes 73732
  63.8 31.0 %collective-permute-start = (bf16[512,4,1,48]{0,3,2,1:T(8,128)(2,1)S(1)}, bf16[512,4,1,48]{0,3,2,1:T(8,128)(2,1)}, u32[]{:S(2)}, u32[]{:S(2)}) collective-permute-start(bf16[512,4,1,48]{0,3,2,1:T(8,128)(2,1)S(1)} %copy.131), channel_id=1, source_target_pairs={{0,4},{4,8},{8,12},{12,0},{1,5},{5,9},{9,13},{13,1},{2,6},{6,10},{... | collective-permute-start | bytes 589832 | tf_op jit(solution)/shard_map/ppermute | solution.py:16
  67.9 29.0 %collective-permute-start.1 = (bf16[512,4,1,48]{0,3,2,1:T(8,128)(2,1)}, bf16[512,4,1,48]{0,3,2,1:T(8,128)(2,1)}, u32[]{:S(2)}, u32[]{:S(2)}) collective-permute-start(bf16[512,4,1,48]{0,3,2,1:T(8,128)(2,1)} %copy.132), channel_id=1, source_target_pairs={{4,0},{8,4},{12,8},{0,12},{5,1},{9,5},{13,9},{1,13},{6,2},{10,6},{... | collective-permute-start | bytes 589832 | tf_op jit(solution)/shard_map/ppermute | solution.py:18
  72.5 1.0 copy-start.6
  72.5 0.9 copy-start.8
  72.7 10.2 %copy-start.5 = (bf16[16,27,512]{2,0,1:T(8,128)(2,1)S(1)}, bf16[16,27,512]{2,0,1:T(8,128)(2,1)}, u32[]{:S(2)}) copy-start(bf16[16,27,512]{2,0,1:T(8,128)(2,1)} %param.4) | copy-start | bytes 1327108
  73.4 10.6 %collective-permute-start.6 = (bf16[16,4,6,1]{3,2,1,0:T(8,128)(2,1)}, bf16[16,4,6,1]{3,2,1,0:T(8,128)(2,1)S(1)}, u32[]{:S(2)}, u32[]{:S(2)}) collective-permute-start(bf16[16,4,6,1]{3,2,1,0:T(8,128)(2,1)} %get-tuple-element.16), channel_id=1, source_target_pairs={{0,1},{1,2},{2,3},{3,0},{4,5},{5,6},{6,7},{7,4},{8,9},{9,10},{10,1... | collective-permute-start | bytes 2312 | tf_op jit(solution)/shard_map/ppermute | solution.py:16
  76.6 7.5 %collective-permute-start.7 = (bf16[16,4,6,1]{3,2,1,0:T(8,128)(2,1)}, bf16[16,4,6,1]{3,2,1,0:T(8,128)(2,1)}, u32[]{:S(2)}, u32[]{:S(2)}) collective-permute-start(bf16[16,4,6,1]{3,2,1,0:T(8,128)(2,1)} %get-tuple-element.17), channel_id=1, source_target_pairs={{1,0},{2,1},{3,2},{0,3},{5,4},{6,5},{7,6},{4,7},{9,8},{10,9},{11,1... | collective-permute-start | bytes 2312 | tf_op jit(solution)/shard_map/ppermute | solution.py:18
  80.1 3.9 %copy-start.7 = (bf16[16,4,1,48]{3,2,1,0:T(2,128)(2,1)S(1)}, bf16[16,4,1,48]{3,2,1,0:T(2,128)(2,1)}, u32[]{:S(2)}) copy-start(bf16[16,4,1,48]{3,2,1,0:T(2,128)(2,1)} %copy-done.6) | copy-start | bytes 18436
  80.1 3.9 %copy-start.9 = (bf16[16,4,1,48]{3,2,1,0:T(2,128)(2,1)S(1)}, bf16[16,4,1,48]{3,2,1,0:T(2,128)(2,1)}, u32[]{:S(2)}) copy-start(bf16[16,4,1,48]{3,2,1,0:T(2,128)(2,1)} %copy-done.8) | copy-start | bytes 18436
  105.7 4.6 %copy-start = (bf16[512,4,6,48]{3,2,1,0:T(8,128)(2,1)}, bf16[512,4,6,48]{3,2,1,0:T(8,128)(2,1)S(1)}, u32[]{:S(2)}) copy-start(bf16[512,4,6,48]{3,2,1,0:T(8,128)(2,1)S(1)} %pad_maximum_fusion) | copy-start | bytes 3538948
  115.6 19.5 %collective-permute-start.2 = (bf16[512,4,6,1]{0,1,3,2:T(4,128)(2,1)S(1)}, bf16[512,4,6,1]{0,1,3,2:T(4,128)(2,1)S(1)}, u32[]{:S(2)}, u32[]{:S(2)}) collective-permute-start(bf16[512,4,6,1]{0,1,3,2:T(4,128)(2,1)S(1)} %copy.135), channel_id=1, source_target_pairs={{0,1},{1,2},{2,3},{3,0},{4,5},{5,6},{6,7},{7,4},{8,9},{9,10},{10,1... | collective-permute-start | bytes 73736 | tf_op jit(solution)/shard_map/ppermute | solution.py:16
  117.6 10.3 %copy-start.1 = (bf16[512,4,4,48]{0,3,2,1:T(8,128)(2,1)S(1)}, bf16[512,4,4,48]{0,3,2,1:T(8,128)(2,1)}, u32[]{:S(2)}) copy-start(bf16[512,4,4,48]{0,3,2,1:T(8,128)(2,1)} %copy.167) | copy-start | bytes 2359300
  117.6 10.3 %copy-start.2 = (bf16[432,768]{1,0:T(8,128)(2,1)S(1)}, bf16[432,768]{1,0:T(8,128)(2,1)}, u32[]{:S(2)}) copy-start(bf16[432,768]{1,0:T(8,128)(2,1)} %reshape.38) | copy-start | bytes 1990660
  123.1 12.0 %collective-permute-start.3 = (bf16[512,4,6,1]{0,1,3,2:T(4,128)(2,1)S(1)}, bf16[512,4,6,1]{0,1,3,2:T(4,128)(2,1)S(1)}, u32[]{:S(2)}, u32[]{:S(2)}) collective-permute-start(bf16[512,4,6,1]{0,1,3,2:T(4,128)(2,1)S(1)} %copy.136), channel_id=1, source_target_pairs={{1,0},{2,1},{3,2},{0,3},{5,4},{6,5},{7,6},{4,7},{9,8},{10,9},{11,1... | collective-permute-start | bytes 73736 | tf_op jit(solution)/shard_map/ppermute | solution.py:18
  137.9 2.6 %copy-start.3 = (bf16[432,512]{1,0:T(8,128)(2,1)S(1)}, bf16[432,512]{1,0:T(8,128)(2,1)}, u32[]{:S(2)}) copy-start(bf16[432,512]{1,0:T(8,128)(2,1)} %reshape.36) | copy-start | bytes 1327108
Sparse Core Ops, SparseCore 0:
  129.5 108.0 all-reduce.3
where the time goes:
time: 249 us; the launch traced here: 247 us
  waiting for transfers between devices  79.7 us (32%)
  local copies, waits for them, and re-layouts  63.9 us (26%)
  blocking collectives  43.6 us (18%)
  starting transfers between devices  27.3 us (11%)
  between operations  14.4 us (6%)
  other arithmetic  13.9 us (6%)
  matrix products  4.33 us (2%)
    psum x1, waiting for transfers between devices, body(): summed = lax.psum(partial_grad, ('lat', 'lon'))  79.7 us
    all_gather x1, blocking collectives, body(): grad_inner = lax.all_gather(out_grad, 'ch', axis=0, tiled=True)  43.6 us
    slice x6, local copies, waits for them, and re-layouts, padded_2(): lax.slice_in_dim(cells, cells.shape[dim] - width, cells.shape[dim], axis=...  16.3 us
    ppermute x4, starting transfers between devices, padded_2(): lax.ppermute(head, axis, [((i + 1) % count, i) for i in range(count)])  16.2 us
    ppermute x4, starting transfers between devices, padded_2(): lax.ppermute(tail, axis, [(i, (i + 1) % count) for i in range(count)])  11.1 us
    reshape x1, local copies, waits for them, and re-layouts, body(): products = products.reshape((chans, 27) + tuple(grad_pad.shape[1:]))  9.47 us
    slice x2, local copies, waits for them, and re-layouts, padded_2(): head = lax.slice_in_dim(cells, 0, width, axis=dim)  7.66 us
    concatenate x1, local copies, waits for them, and re-layouts, padded_2(): jnp.concatenate([lax.ppermute(tail, axis, [(i, (i + 1) % count) for i in...  5.73 us
  transfers between devices with their start and end apart: 9, of which 1 were waited for; matrix products, arithmetic and copies ran while one was open for 24% of the time, Pallas kernels for 0%

commit v1 on v0

v1 whole, which is shorter than its diff:
```python
import math

import jax
import jax.numpy as jnp
from jax import lax
from jax.experimental import pallas as pl
from jax.experimental.pallas import tpu as pltpu
from jax.sharding import PartitionSpec as P

MESH = pl.DeviceIdType.MESH
F32 = jnp.float32
BF16 = jnp.bfloat16

CH = 16
LEV = 4
ROWS = 4
COLS = 48
GROUPS = ROWS * LEV
CELLS = GROUPS * COLS
HALF = CELLS // 2
SIDE = 4
TAPS = 27
PER = 7
PART = 56
FILT = 512
STEP_LAT = LEV * COLS
NEAR = [(a, b) for a in (-1, 0, 1) for b in (-1, 0, 1) if (a, b) != (0, 0)]


def roll(values, shift):
    return pltpu.roll(values, shift % values.shape[1], axis=1)


def iota(shape, dim):
    return lax.broadcasted_iota(jnp.int32, shape, dim)


def group_of(lane):
    return lax.shift_right_logical(lane * 1366, 16)


def lane_places(rows):
    lane = iota((rows, CELLS), 1)
    group = group_of(lane)
    return lax.shift_right_logical(group, 2), group & 3, lane - group * COLS


def spread_matrix():
    lane = iota((COLS, CELLS), 1)
    return jnp.where(lane - group_of(lane) * COLS == iota((COLS, CELLS), 0), 1.0, 0.0).astype(BF16)


def keep_matrix():
    row = iota((GROUPS, CELLS), 0)
    group = (row & 3) * 4 + lax.shift_right_logical(row, 2)
    return jnp.where(group_of(iota((GROUPS, CELLS), 1)) == group, 1.0, 0.0).astype(F32)


def to_lanes(block, spread, keep):
    wide = jnp.dot(block, spread, preferred_element_type=F32).reshape(CH, GROUPS, CELLS)
    wide = (wide * keep[None]).reshape(CH * GROUPS, CELLS).astype(BF16)
    shape = (CH, CH * GROUPS)
    pick = jnp.where(lax.shift_right_logical(iota(shape, 1), 4) == iota(shape, 0), 1.0, 0.0).astype(BF16)
    return jnp.dot(pick, wide, preferred_element_type=F32).astype(BF16)


def from_lanes(cells, spread, keep):
    shape = (CH * GROUPS, CH)
    pick = jnp.where(lax.shift_right_logical(iota(shape, 0), 4) == iota(shape, 1), 1.0, 0.0).astype(BF16)
    wide = jnp.dot(pick, cells, preferred_element_type=F32).reshape(CH, GROUPS, CELLS)
    wide = (wide * keep[None]).reshape(CH * GROUPS, CELLS).astype(BF16)
    return lax.dot_general(
        wide, spread, (((1,), (1,)), ((), ())), preferred_element_type=F32
    ).astype(BF16)


def moved_row(near, d_lat, places):
    row, _, _ = places
    moved = {}
    for b in (-1, 0, 1):
        if d_lat == 0:
            moved[b] = near(0, b)
        elif d_lat == 1:
            moved[b] = roll(jnp.where(row == 0, near(1, b), near(0, b)), -STEP_LAT)
        else:
            moved[b] = roll(jnp.where(row == ROWS - 1, near(-1, b), near(0, b)), STEP_LAT)
    return moved


def taps_of_row(moved, places):
    _, level, col = places
    for d_lon in (-1, 0, 1):
        if d_lon == 0:
            base = moved[0]
        elif d_lon == 1:
            base = jnp.where(col == COLS - 1, roll(moved[1], COLS - 1), roll(moved[0], -1))
        else:
            base = jnp.where(col == 0, roll(moved[-1], 1 - COLS), roll(moved[0], 1))
        yield 0, d_lon, base
        yield 1, d_lon, jnp.where(level < LEV - 1, roll(base, -COLS), 0.0)
        yield -1, d_lon, jnp.where(level > 0, roll(base, COLS), 0.0)


def shifted_sums(product, places):
    row, level, col = places
    own = {}
    east = {}
    west = {}
    for d_lat in (-1, 0, 1):
        q = {}
        for d_lon in (-1, 0, 1):
            tap = (d_lat + 1) * 3 + d_lon + 1
            q[d_lon] = (
                product(9 + tap)
                + jnp.where(level > 0, roll(product(18 + tap), COLS), 0.0)
                + jnp.where(level < LEV - 1, roll(product(tap), -COLS), 0.0)
            )
        own[d_lat] = (
            q[0]
            + jnp.where(col > 0, roll(q[1], 1), 0.0)
            + jnp.where(col < COLS - 1, roll(q[-1], -1), 0.0)
        )
        east[d_lat] = jnp.where(col == 0, roll(q[1], 1 - COLS), 0.0)
        west[d_lat] = jnp.where(col == COLS - 1, roll(q[-1], COLS - 1), 0.0)
    out = {}
    for b, sums in ((0, own), (1, east), (-1, west)):
        up = roll(sums[1], STEP_LAT)
        down = roll(sums[-1], -STEP_LAT)
        out[0, b] = (
            sums[0] + jnp.where(row > 0, up, 0.0) + jnp.where(row < ROWS - 1, down, 0.0)
        )
        out[1, b] = jnp.where(row == 0, up, 0.0)
        out[-1, b] = jnp.where(row == ROWS - 1, down, 0.0)
    return out


def pack_column(frame):
    low = frame[:, 0:128] + frame[:, 128:256] + frame[:, 256:384]
    high = frame[:, 384:512] + frame[:, 512:640] + frame[:, 640:768]
    return low + roll(high, 1)


def unpack_column(packed, places, at):
    other = roll(packed, -1)
    wide = jnp.concatenate([packed] * 3 + [other] * 3, axis=1)
    return jnp.where(places[2] == at, wide, 0.0)


def kernel(
    nz,
    scale,
    x_ref,
    w_hbm,
    g_ref,
    xg_ref,
    wg_ref,
    field,
    cols,
    gath,
    wts,
    prod,
    part,
    slab,
    got1,
    got2,
    full,
    lat_out,
    lat_in,
    pt_out,
    pt_in,
    w_sem,
    ring_send,
    ring_recv,
    sib_send,
    sib_recv,
    xh_send,
    xh_recv,
    ph_send,
    ph_recv,
    st_send,
    st_recv,
):
    ch = lax.axis_index("ch")
    lat = lax.axis_index("lat")
    lon = lax.axis_index("lon")
    z = ch // 2
    core = ch % 2
    sibling = z * 2 + (1 - core)
    here = {"lat": lat, "lon": lon}

    def z_at(step):
        return lax.rem(z + step + nz, nz) * 2 + core

    def side_at(axis, step):
        return lax.rem(here[axis] + step + SIDE, SIDE)

    fetch = pltpu.make_async_copy(w_hbm, wts, w_sem)
    fetch.start()

    barrier = pltpu.get_barrier_semaphore()
    peers = [{"ch": z_at(1)}, {"ch": z_at(-1)}, {"ch": sibling}]
    for axis in ("lat", "lon"):
        peers += [{axis: side_at(axis, step)} for step in (1, 2, 3)]
    peers += [
        {"lat": side_at("lat", a), "lon": side_at("lon", b)} for a in (-1, 1) for b in (-1, 1)
    ]
    for peer in peers:
        pl.semaphore_signal(barrier, inc=1, device_id=peer, device_id_type=MESH)

    places = lane_places(CH)
    spread = spread_matrix()
    keep = keep_matrix()
    gath[ch] = to_lanes(g_ref[...], spread, keep)
    field[4] = to_lanes(x_ref[...], spread, keep)

    pl.semaphore_wait(barrier, len(peers))

    sends = []

    def send(src, dst, send_sem, recv_sem, peer):
        copy = pltpu.make_async_remote_copy(
            src_ref=src,
            dst_ref=dst,
            send_sem=send_sem,
            recv_sem=recv_sem,
            device_id=peer,
            device_id_type=MESH,
        )
        copy.start()
        sends.append(copy)

    def arrived(dst, send_sem, recv_sem, peer):
        pltpu.make_async_remote_copy(
            src_ref=dst,
            dst_ref=dst,
            send_sem=send_sem,
            recv_sem=recv_sem,
            device_id=peer,
            device_id_type=MESH,
        ).wait_recv()

    def onward(way, step):
        sign = 1 if way == 0 else -1
        slot = z_at(-sign * (step - 1))
        send(
            gath.at[slot],
            gath.at[slot],
            ring_send.at[way, step - 1],
            ring_recv.at[way, step - 1],
            {"ch": z_at(sign)},
        )

    def across(order, step):
        slot = z_at(step)
        send(gath.at[slot], gath.at[slot], sib_send.at[order], sib_recv.at[order], {"ch": sibling})

    reach = (nz // 2, (nz - 1) // 2)

    onward(0, 1)
    onward(1, 1)
    across(0, 0)
    for n, (a, b) in enumerate(NEAR):
        send(
            field.at[4],
            field.at[(1 - a) * 3 + 1 - b],
            xh_send.at[n],
            xh_recv.at[n],
            {"lat": side_at("lat", a), "lon": side_at("lon", b)},
        )

    south = jnp.where(lat > 0, 1.0, 0.0).astype(F32)
    north = jnp.where(lat < SIDE - 1, 1.0, 0.0).astype(F32)
    inside = {-1: south, 1: north}

    def near(a, b):
        block = field[(a + 1) * 3 + b + 1].astype(F32)
        return block if a == 0 else block * inside[a]

    def build(d_lat):
        for d_lev, d_lon, value in taps_of_row(moved_row(near, d_lat, places), places):
            tap = (d_lev + 1) * 9 + (d_lat + 1) * 3 + d_lon + 1
            value = value.astype(BF16)
            for side in range(2):
                at = (tap // PER * 2 + side) * PART + tap % PER * 8
                cols[at : at + 8, :] = value[side * 8 : side * 8 + 8]

    def clear_spare():
        for side in range(2):
            at = (3 * 2 + side) * PART + 6 * 8
            cols[at : at + 8, :] = jnp.zeros((8, CELLS), BF16)

    def wait_field():
        for n, (a, b) in enumerate(NEAR):
            arrived(
                field.at[(1 - a) * 3 + 1 - b],
                xh_send.at[n],
                xh_recv.at[n],
                {"lat": side_at("lat", -a), "lon": side_at("lon", -b)},
            )

    order = 1
    for step in range(1, reach[0] + 1):
        for way in (0, 1):
            if step > reach[way]:
                continue
            sign = 1 if way == 0 else -1
            slot = z_at(-sign * step)
            arrived(
                gath.at[slot],
                ring_send.at[way, step - 1],
                ring_recv.at[way, step - 1],
                {"ch": z_at(-sign)},
            )
            if step < reach[way]:
                onward(way, step + 1)
            across(order, -sign * step)
            order += 1
        if step == 1:
            clear_spare()
        if step == 2:
            wait_field()
            build(0)
        if step == 3:
            build(1)
        if step == 4:
            build(-1)
    order = 0
    for step in [0] + [s for n in range(1, reach[0] + 1) for s in (-n, n) if s != reach[0]]:
        slot = lax.rem(z + step + nz, nz) * 2 + (1 - core)
        arrived(gath.at[slot], sib_send.at[order], sib_recv.at[order], {"ch": sibling})
        order += 1

    axes = (("lat", "lon"), ("lon", "lat"))

    def sum_half(half):
        filters = gath[half * 16 : half * 16 + 16].reshape(FILT // 2, CELLS)
        sums = lax.dot_general(
            cols[...], filters, (((1,), (1,)), ((), ())), preferred_element_type=F32
        )
        for n in range(2):
            part[2 * half + n] = sums[:, n * 128 : n * 128 + 128].reshape(SIDE, 2, PART, 128)

    def stage_send(stage, half, src, dst):
        axis = axes[half][0 if stage in (0, 3) else 1]
        for d in (1, 3, 2):
            peer = side_at(axis, d)
            send(
                src(peer),
                dst(d - 1),
                st_send.at[stage, half, d - 1],
                st_recv.at[stage, half, d - 1],
                {axis: peer},
            )

    def stage_wait(stage, half, dst):
        axis = axes[half][0 if stage in (0, 3) else 1]
        for d in (1, 3, 2):
            peer = side_at(axis, -d)
            arrived(
                dst(d - 1, peer),
                st_send.at[stage, half, d - 1],
                st_recv.at[stage, half, d - 1],
                {axis: peer},
            )

    for half in range(2):
        sum_half(half)
        stage_send(
            0,
            half,
            lambda peer: part.at[pl.ds(2 * half, 2), peer],
            lambda n: got1.at[half, n],
        )

    fetch.wait()
    prod[...] = jnp.dot(
        wts[...].reshape(TAPS * CH, FILT),
        gath[...].reshape(FILT, CELLS),
        preferred_element_type=F32,
    )
    sums = shifted_sums(lambda tap: prod[tap * CH : tap * CH + CH, :], places)
    mine = sums[0, 0]
    lat_out[0] = sums[1, 0][:, 0:256]
    lat_out[1] = sums[-1, 0][:, CELLS - 256 : CELLS]
    columns = [(a, b) for a in (-1, 0, 1) for b in (-1, 1)]
    for n, at in enumerate(columns):
        pt_out[n] = pack_column(sums[at])
    prod[0:CH, :] = mine
    for n, a in enumerate((1, -1)):
        send(
            lat_out.at[n],
            lat_in.at[n],
            ph_send.at[n],
            ph_recv.at[n],
            {"lat": side_at("lat", a)},
        )
    for n, (a, b) in enumerate(columns):
        send(
            pt_out.at[n],
            pt_in.at[n],
            ph_send.at[2 + n],
            ph_recv.at[2 + n],
            {"lat": side_at("lat", a), "lon": side_at("lon", b)},
        )

    for half in range(2):
        first = here[axes[half][0]]
        stage_wait(0, half, lambda n, peer: got1.at[half, n])
        for v in range(SIDE):
            slab[half, v] = (
                part[2 * half + v // 2, first, v % 2]
                + got1[half, 0, v // 2, v % 2]
                + got1[half, 1, v // 2, v % 2]
                + got1[half, 2, v // 2, v % 2]
            )
        stage_send(
            1,
            half,
            lambda peer: slab.at[half, peer],
            lambda n: got2.at[half, n],
        )

    for n, a in enumerate((1, -1)):
        arrived(
            lat_in.at[n], ph_send.at[n], ph_recv.at[n], {"lat": side_at("lat", -a)}
        )
    for n, (a, b) in enumerate(columns):
        arrived(
            pt_in.at[n],
            ph_send.at[2 + n],
            ph_recv.at[2 + n],
            {"lat": side_at("lat", -a), "lon": side_at("lon", -b)},
        )
    total = prod[0:CH, :]
    total += jnp.concatenate(
        [lat_in[0] * south, jnp.zeros((CH, CELLS - 512), F32), lat_in[1] * north], axis=1
    )
    for n, (a, b) in enumerate(columns):
        packed = pt_in[n]
        if a != 0:
            packed = packed * (south if a == 1 else north)
        total += unpack_column(packed, places, 0 if b == 1 else COLS - 1)
    xg_ref[...] = from_lanes(total.astype(BF16), spread, keep)

    for half in range(2):
        first, second = here[axes[half][0]], here[axes[half][1]]
        stage_wait(1, half, lambda n, peer: got2.at[half, n])
        full[2 * half + second // 2, first, second % 2] = (
            slab[half, second] + got2[half, 0] + got2[half, 1] + got2[half, 2]
        ) * scale
        chunk = full.at[2 * half + second // 2, first, second % 2]
        stage_send(2, half, lambda peer: chunk, lambda n: chunk)
    for half in range(2):
        first = here[axes[half][0]]
        stage_wait(
            2, half, lambda n, peer: full.at[2 * half + peer // 2, first, peer % 2]
        )
        block = full.at[pl.ds(2 * half, 2), first]
        stage_send(3, half, lambda peer: block, lambda n: block)
    for half in range(2):
        stage_wait(3, half, lambda n, peer: full.at[pl.ds(2 * half, 2), peer])
    for tap in range(TAPS):
        for n in range(FILT // 128):
            for side in range(2):
                wg_ref[tap, side * 8 : side * 8 + 8, n * 128 : n * 128 + 128] = full[
                    n, tap // PER, side, tap % PER * 8 : tap % PER * 8 + 8, :
                ]
    for copy in sends:
        copy.wait_send()


def body(inputs, weights, out_grad):
    nz = lax.axis_size("ch") // 2
    cells = CELLS * lax.axis_size("lat") * lax.axis_size("lon")
    dma = pltpu.SemaphoreType.DMA
    vmem = pl.BlockSpec(memory_space=pltpu.VMEM)
    input_grad, weight_grad = pl.pallas_call(
        lambda *refs: kernel(nz, 1.0 / math.sqrt(cells), *refs),
        out_shape=(
            jax.ShapeDtypeStruct((CH * GROUPS, COLS), BF16),
            jax.ShapeDtypeStruct((TAPS, CH, FILT), F32),
        ),
        in_specs=[vmem, pl.BlockSpec(memory_space=pl.ANY), vmem],
        out_specs=(vmem, vmem),
        scratch_shapes=[
            pltpu.VMEM((9, CH, CELLS), BF16),
            pltpu.VMEM((SIDE * 2 * PART, CELLS), BF16),
            pltpu.VMEM((2 * nz, CH, CELLS), BF16),
            pltpu.VMEM((TAPS, CH, FILT), BF16),
            pltpu.VMEM((TAPS * CH, CELLS), F32),
            pltpu.VMEM((4, SIDE, 2, PART, 128), F32),
            pltpu.VMEM((2, SIDE, PART, 128), F32),
            pltpu.VMEM((2, 3, 2, 2, PART, 128), F32),
            pltpu.VMEM((2, 3, PART, 128), F32),
            pltpu.VMEM((4, SIDE, 2, PART, 128), F32),
            pltpu.VMEM((2, CH, 256), F32),
            pltpu.VMEM((2, CH, 256), F32),
            pltpu.VMEM((6, CH, 128), F32),
            pltpu.VMEM((6, CH, 128), F32),
            dma,
            dma((2, nz // 2)),
            dma((2, nz // 2)),
            dma((nz,)),
            dma((nz,)),
            dma((8,)),
            dma((8,)),
            dma((8,)),
            dma((8,)),
            dma((4, 2, 3)),
            dma((4, 2, 3)),
        ],
        compiler_params=pltpu.CompilerParams(
            collective_id=0, has_side_effects=True, vmem_limit_bytes=40 << 20
        ),
    )(
        inputs.reshape(CH * GROUPS, COLS),
        jnp.transpose(weights, (1, 0, 2)),
        out_grad.reshape(CH * GROUPS, COLS),
    )
    return input_grad.reshape(inputs.shape), jnp.transpose(weight_grad, (1, 0, 2))


def solution(mesh):
    in_specs = (P("ch", None, "lat", "lon"), P("ch", None, None), P("ch", None, "lat", "lon"))
    out_specs = (P("ch", None, "lat", "lon"), P("ch", None, None))
    return jax.shard_map(body, mesh=mesh, in_specs=in_specs, out_specs=out_specs, check_vma=False)
```

time: 249 us -> 68.4 us (0.27)
  waiting for transfers between devices: 79.7 us -> 0 us
  Pallas kernels: 0 us -> 63.1 us
  local copies, waits for them, and re-layouts: 63.9 us -> 4.23 us
  blocking collectives: 43.6 us -> 0 us
  starting transfers between devices: 27.3 us -> 0 us
  other arithmetic: 13.9 us -> 0 us
  between operations: 14.4 us -> 0.65 us
  matrix products: 4.33 us -> 0 us
    psum x1 -> x0, waiting for transfers between devices: 79.7 us -> none  [body(): summed = lax.psum(partial_grad, ('lat', 'lon'))]
    pallas_call x0 -> x1, Pallas kernels: none -> 63.1 us  [body(): pl.pallas_call(lambda *refs: kernel(nz, 1.0 / math.sqrt(cells), *refs), o...]
    all_gather x1 -> x0, blocking collectives: 43.6 us -> none  [body(): grad_inner = lax.all_gather(out_grad, 'ch', axis=0, tiled=True)]
    ppermute x8 -> x0, starting transfers between devices: 27.2 us -> none  [the longest x4 16.2 us: padded_2(): lax.ppermute(head, axis, [((i + 1) % count, i) for i in range(count)])]
    slice x8 -> x0, local copies, waits for them, and re-layouts: 23.9 us -> none  [the longest x6 16.3 us: padded_2(): lax.slice_in_dim(cells, cells.shape[dim] - width, cells.shape[dim], axis=...]
    reshape x5 -> x0, local copies, waits for them, and re-layouts: 17.9 us -> none  [the longest x1 9.47 us: body(): products = products.reshape((chans, 27) + tuple(grad_pad.shape[1:]))]
    concatenate x1 -> x0, local copies, waits for them, and re-layouts: 5.73 us -> none  [padded_2(): jnp.concatenate([lax.ppermute(tail, axis, [(i, (i + 1) % count) for i in...]
    concatenate x2 -> x0, other arithmetic: 5.54 us -> none  [padded_2(): jnp.concatenate([lax.ppermute(tail, axis, [(i, (i + 1) % count) for i in...]
  transfers between devices with their start and end apart: 9 -> 0, of which waited for: 1 -> 0; matrix products, arithmetic and copies ran while one was open for 24% -> 0% of each run, Pallas kernels for 0% -> 0%
where the time goes in v1:
time: 68.4 us; the launch traced here: 68 us
  Pallas kernels  63.1 us (92%)
  local copies, waits for them, and re-layouts  4.23 us (6%)
    pallas_call x1, Pallas kernels, body(): pl.pallas_call(lambda *refs: kernel(nz, 1.0 / math.sqrt(cells), *refs), o...  63.1 us
    unnamed x8, local copies, waits for them, and re-layouts  4.23 us

profile of v1, /device:TPU:1, one launch (start us, length us, event | category | flops | bytes accessed | tf_op | source)
XLA Modules:
  0.0 68.0 jit_solution(14803886268662884885)
XLA Ops:
  0.6 0.0 copy-start
  0.6 1.0 %copy-done = bf16[16,27,512]{2,0,1:T(8,128)(2,1)S(1)} copy-done((bf16[16,27,512]{2,0,1:T(8,128)(2,1)S(1)}, bf16[16,27,512]{2,0,1:T(8,128)(2,1)}, u32[]{:S(2)}) %copy-start) | copy-done | bytes 442392
  1.6 0.0 copy-start.1
  1.6 0.8 %copy-done.1 = bf16[16,4,4,48]{3,2,1,0:T(4,128)(2,1)S(1)} copy-done((bf16[16,4,4,48]{3,2,1,0:T(4,128)(2,1)S(1)}, bf16[16,4,4,48]{3,2,1,0:T(4,128)(2,1)}, u32[]{:S(2)}) %copy-start.1) | copy-done | bytes 24600
  2.5 0.0 copy-start.2
  2.5 0.8 %copy-done.2 = bf16[16,4,4,48]{3,2,1,0:T(4,128)(2,1)S(1)} copy-done((bf16[16,4,4,48]{3,2,1,0:T(4,128)(2,1)S(1)}, bf16[16,4,4,48]{3,2,1,0:T(4,128)(2,1)}, u32[]{:S(2)}) %copy-start.2) | copy-done | bytes 24600
  3.3 63.1 %shard_map.50 = (bf16[256,48]{1,0:T(8,128)(2,1)S(1)}, f32[27,16,512]{2,1,0:T(8,128)S(1)}) custom-call(bf16[256,48]{1,0:T(8,128)(2,1)S(1)} %bitcast.7, bf16[27,16,512]{2,1,0:T(8,128)(2,1)S(1)} %bitcast.6, bf16[256,48]{1,0:T(8,128)(2,1)S(1)} %bitcast.8), custom_call_target="tpu_custom_call" | custom-call | tf_op jit(solution)/shard_map/pallas_call | solution.py:477
  66.5 0.6 copy.7
  67.1 0.9 %copy.8 = f32[16,27,512]{2,0,1:T(8,128)} copy(f32[16,27,512]{2,0,1:T(8,128)S(1)} %bitcast.5) | data formatting | bytes 1769472
Async XLA Ops:
  0.6 1.0 %copy-start = (bf16[16,27,512]{2,0,1:T(8,128)(2,1)S(1)}, bf16[16,27,512]{2,0,1:T(8,128)(2,1)}, u32[]{:S(2)}) copy-start(bf16[16,27,512]{2,0,1:T(8,128)(2,1)} %param.4) | copy-start | bytes 1327108
  1.6 0.8 %copy-start.1 = (bf16[16,4,4,48]{3,2,1,0:T(4,128)(2,1)S(1)}, bf16[16,4,4,48]{3,2,1,0:T(4,128)(2,1)}, u32[]{:S(2)}) copy-start(bf16[16,4,4,48]{3,2,1,0:T(4,128)(2,1)} %param.3) | copy-start | bytes 73732
  2.5 0.8 %copy-start.2 = (bf16[16,4,4,48]{3,2,1,0:T(4,128)(2,1)S(1)}, bf16[16,4,4,48]{3,2,1,0:T(4,128)(2,1)}, u32[]{:S(2)}) copy-start(bf16[16,4,4,48]{3,2,1,0:T(4,128)(2,1)} %param.5) | copy-start | bytes 73732

commit v2 on v1

v2 whole, which is shorter than its diff:
```python
import math

import jax
import jax.numpy as jnp
from jax import lax
from jax.experimental import pallas as pl
from jax.experimental.pallas import tpu as pltpu
from jax.sharding import PartitionSpec as P

MESH = pl.DeviceIdType.MESH
F32 = jnp.float32
BF16 = jnp.bfloat16

CH = 16
LEV = 4
ROWS = 4
COLS = 48
GROUPS = ROWS * LEV
CELLS = GROUPS * COLS
SIDE = 4
TAPS = 27
PER = 7
PART = PER * CH
FILT = 512
STEP_LAT = LEV * COLS
TOP = 2.0**30
TINY = 1e-28
VMEM_BYTES = 60 << 20
OTHERS = sorted(
    ((a, b) for a in range(SIDE) for b in range(SIDE) if (a, b) != (0, 0)),
    key=lambda at: -(min(at[0], SIDE - at[0]) + min(at[1], SIDE - at[1])),
)
NEAR = [(a, b) for a in (-1, 0, 1) for b in (-1, 0, 1) if (a, b) != (0, 0)]


def roll(values, shift):
    return pltpu.roll(values, shift % values.shape[1], axis=1)


def iota(shape, dim):
    return lax.broadcasted_iota(jnp.int32, shape, dim)


def group_of(lane):
    return lax.shift_right_logical(lane * 1366, 16)


def lane_places(rows):
    lane = iota((rows, CELLS), 1)
    group = group_of(lane)
    return lax.shift_right_logical(group, 2), group & 3, lane - group * COLS


def spread_matrix():
    lane = iota((COLS, CELLS), 1)
    return jnp.where(lane - group_of(lane) * COLS == iota((COLS, CELLS), 0), 1.0, 0.0).astype(BF16)


def keep_matrix():
    row = iota((GROUPS, CELLS), 0)
    group = (row & 3) * 4 + lax.shift_right_logical(row, 2)
    return jnp.where(group_of(iota((GROUPS, CELLS), 1)) == group, 1.0, 0.0).astype(F32)


def to_lanes(block, spread, keep):
    wide = jnp.dot(block, spread, preferred_element_type=F32).reshape(CH, GROUPS, CELLS)
    wide = (wide * keep[None]).reshape(CH * GROUPS, CELLS).astype(BF16)
    shape = (CH, CH * GROUPS)
    pick = jnp.where(lax.shift_right_logical(iota(shape, 1), 4) == iota(shape, 0), 1.0, 0.0).astype(BF16)
    return jnp.dot(pick, wide, preferred_element_type=F32).astype(BF16)


def from_lanes(cells, spread, keep):
    shape = (CH * GROUPS, CH)
    pick = jnp.where(lax.shift_right_logical(iota(shape, 0), 4) == iota(shape, 1), 1.0, 0.0).astype(BF16)
    wide = jnp.dot(pick, cells, preferred_element_type=F32).reshape(CH, GROUPS, CELLS)
    wide = (wide * keep[None]).reshape(CH * GROUPS, CELLS).astype(BF16)
    return lax.dot_general(
        wide, spread, (((1,), (1,)), ((), ())), preferred_element_type=F32
    ).astype(BF16)


def moved_row(near, d_lat, places):
    row, _, _ = places
    moved = {}
    for b in (-1, 0, 1):
        if d_lat == 0:
            moved[b] = near(0, b)
        elif d_lat == 1:
            moved[b] = roll(jnp.where(row == 0, near(1, b), near(0, b)), -STEP_LAT)
        else:
            moved[b] = roll(jnp.where(row == ROWS - 1, near(-1, b), near(0, b)), STEP_LAT)
    return moved


def taps_of_row(moved, places):
    _, level, col = places
    for d_lon in (-1, 0, 1):
        if d_lon == 0:
            base = moved[0]
        elif d_lon == 1:
            base = jnp.where(col == COLS - 1, roll(moved[1], COLS - 1), roll(moved[0], -1))
        else:
            base = jnp.where(col == 0, roll(moved[-1], 1 - COLS), roll(moved[0], 1))
        yield 0, d_lon, base
        yield 1, d_lon, jnp.where(level < LEV - 1, roll(base, -COLS), 0.0)
        yield -1, d_lon, jnp.where(level > 0, roll(base, COLS), 0.0)


def shifted_sums(product, places):
    row, level, col = places
    own = {}
    east = {}
    west = {}
    for d_lat in (-1, 0, 1):
        q = {}
        for d_lon in (-1, 0, 1):
            tap = (d_lat + 1) * 3 + d_lon + 1
            q[d_lon] = (
                product(9 + tap)
                + jnp.where(level > 0, roll(product(18 + tap), COLS), 0.0)
                + jnp.where(level < LEV - 1, roll(product(tap), -COLS), 0.0)
            )
        own[d_lat] = (
            q[0]
            + jnp.where(col > 0, roll(q[1], 1), 0.0)
            + jnp.where(col < COLS - 1, roll(q[-1], -1), 0.0)
        )
        east[d_lat] = jnp.where(col == 0, roll(q[1], 1 - COLS), 0.0)
        west[d_lat] = jnp.where(col == COLS - 1, roll(q[-1], COLS - 1), 0.0)
    out = {}
    for b, sums in ((0, own), (1, east), (-1, west)):
        up = roll(sums[1], STEP_LAT)
        down = roll(sums[-1], -STEP_LAT)
        out[0, b] = (
            sums[0] + jnp.where(row > 0, up, 0.0) + jnp.where(row < ROWS - 1, down, 0.0)
        )
        out[1, b] = jnp.where(row == 0, up, 0.0)
        out[-1, b] = jnp.where(row == ROWS - 1, down, 0.0)
    return out


def pack_column(frame):
    low = frame[:, 0:128] + frame[:, 128:256] + frame[:, 256:384]
    high = frame[:, 384:512] + frame[:, 512:640] + frame[:, 640:768]
    return low + roll(high, 1)


def unpack_column(packed, places, at):
    other = roll(packed, -1)
    wide = jnp.concatenate([packed] * 3 + [other] * 3, axis=1)
    return jnp.where(places[2] == at, wide, 0.0)


def encode(values, scale):
    scaled = values * scale
    square = scaled * scaled
    return (square * scaled * jnp.abs(scaled)).astype(BF16)


def decode(codes):
    inverse = 1.0 / codes[PART:, :].astype(F32)
    power = codes[:PART, :].astype(F32).reshape(PART // 8, 8, 128)
    root = lax.rsqrt(lax.rsqrt(jnp.abs(power))) * inverse[None]
    return jnp.where(power < 0, -root, root).reshape(PART, 128)


def scale_for(largest):
    return (TOP / jnp.maximum(largest, TINY)).astype(BF16)


def kernel(
    nz,
    scale,
    x_hbm,
    w_hbm,
    g_hbm,
    xg_ref,
    wg_ref,
    x_own,
    g_own,
    field,
    cols,
    gath,
    wts,
    prod,
    part,
    codes,
    got,
    full,
    lat_out,
    lat_in,
    pt_out,
    pt_in,
    in_sem,
    z_send,
    z_recv,
    sib_send,
    sib_recv,
    xh_send,
    xh_recv,
    ph_send,
    ph_recv,
    rs_send,
    rs_recv,
    ag_send,
    ag_recv,
):
    ch = lax.axis_index("ch")
    lat = lax.axis_index("lat")
    lon = lax.axis_index("lon")
    z = ch // 2
    core = ch % 2
    sibling = z * 2 + (1 - core)
    here = {"lat": lat, "lon": lon}

    fetches = [
        pltpu.make_async_copy(src, dst, in_sem.at[n])
        for n, (src, dst) in enumerate(((g_hbm, g_own), (x_hbm, x_own), (w_hbm, wts)))
    ]
    for fetch in fetches:
        fetch.start()

    def z_at(step):
        return lax.rem(z + step + nz, nz) * 2 + core

    def side_at(axis, step):
        return lax.rem(here[axis] + step + SIDE, SIDE)

    def plane_at(a, b):
        return {"lat": side_at("lat", a), "lon": side_at("lon", b)}

    barrier = pltpu.get_barrier_semaphore()
    peers = [{"ch": z_at(step)} for step in (4, -4, 3, -3, 2, -2, 1, -1)]
    peers += [{"ch": sibling}] + [plane_at(a, b) for a, b in OTHERS]
    for peer in peers:
        pl.semaphore_signal(barrier, inc=1, device_id=peer, device_id_type=MESH)

    places = lane_places(CH)
    spread = spread_matrix()
    keep = keep_matrix()
    fetches[0].wait()
    gath[ch] = to_lanes(g_own[...], spread, keep)
    fetches[1].wait()
    field[4] = to_lanes(x_own[...], spread, keep)

    pl.semaphore_wait(barrier, len(peers))

    sends = []

    def send(src, dst, send_sem, recv_sem, peer):
        copy = pltpu.make_async_remote_copy(
            src_ref=src,
            dst_ref=dst,
            send_sem=send_sem,
            recv_sem=recv_sem,
            device_id=peer,
            device_id_type=MESH,
        )
        copy.start()
        sends.append(copy)

    def arrived(dst, send_sem, recv_sem, peer):
        pltpu.make_async_remote_copy(
            src_ref=dst,
            dst_ref=dst,
            send_sem=send_sem,
            recv_sem=recv_sem,
            device_id=peer,
            device_id_type=MESH,
        ).wait_recv()

    def to_chip(dist, hop):
        slot = z_at(hop - dist)
        at = (dist + 7) % 16
        send(
            gath.at[slot],
            gath.at[slot],
            z_send.at[at],
            z_recv.at[at],
            {"ch": z_at(hop)},
        )

    def to_sibling(dist):
        slot = z_at(-dist)
        at = (dist + 7) % 16
        send(gath.at[slot], gath.at[slot], sib_send.at[at], sib_recv.at[at], {"ch": sibling})

    def block_here(dist, hop):
        at = (dist + 7) % 16
        arrived(gath.at[z_at(-dist)], z_send.at[at], z_recv.at[at], {"ch": z_at(-hop)})
        to_sibling(dist)

    for dist in (4, -4, 1, -1):
        to_chip(dist, dist)
    to_sibling(0)
    for n, (a, b) in enumerate(NEAR):
        send(
            field.at[4],
            field.at[(1 - a) * 3 + 1 - b],
            xh_send.at[n],
            xh_recv.at[n],
            plane_at(a, b),
        )

    south = jnp.where(lat > 0, 1.0, 0.0).astype(F32)
    north = jnp.where(lat < SIDE - 1, 1.0, 0.0).astype(F32)
    inside = {-1: south, 1: north}

    def near(a, b):
        block = field[(a + 1) * 3 + b + 1].astype(F32)
        return block if a == 0 else block * inside[a]

    def build(d_lat):
        for d_lev, d_lon, value in taps_of_row(moved_row(near, d_lat, places), places):
            tap = (d_lev + 1) * 9 + (d_lat + 1) * 3 + d_lon + 1
            cols[tap * CH : tap * CH + CH, :] = value.astype(BF16)

    cols[TAPS * CH :, :] = jnp.zeros((CH, CELLS), BF16)
    block_here(1, 1)
    to_chip(2, 1)
    block_here(-1, -1)
    to_chip(-2, -1)
    for n, (a, b) in enumerate(NEAR):
        arrived(
            field.at[(1 - a) * 3 + 1 - b], xh_send.at[n], xh_recv.at[n], plane_at(-a, -b)
        )
    build(0)
    block_here(4, 4)
    for hop in (3, 2, 1, -1):
        to_chip(4 + hop, hop)
    block_here(-4, -4)
    for hop in (-3, -2, -1, 1):
        to_chip(-4 + hop, hop)
    way = 4 - 8 * core
    far = z_at(-way)
    send(gath.at[far], gath.at[far], z_send.at[15], z_recv.at[15], {"ch": z_at(way)})
    build(1)
    build(-1)
    for dist, hop in ((2, 1), (-2, -1), (3, -1), (-3, 1), (5, 1), (-5, -1), (6, 2), (-6, -2)):
        block_here(dist, hop)
    for dist, hop in ((7, 3), (-7, -3)):
        block_here(dist, hop)
    block_here(8, way)
    for dist in (0, 1, -1, 4, -4, 2, -2, 3, -3, 5, -5, 6, -6, 7, -7, 8):
        slot = lax.rem(z - dist + nz, nz) * 2 + (1 - core)
        at = (dist + 7) % 16
        arrived(gath.at[slot], sib_send.at[at], sib_recv.at[at], {"ch": sibling})

    largest = None
    for half in range(2):
        filters = gath[half * 16 : half * 16 + 16].reshape(FILT // 2, CELLS)
        sums = lax.dot_general(
            cols[...], filters, (((1,), (1,)), ((), ())), preferred_element_type=F32
        )
        most = jnp.max(jnp.abs(sums), axis=0, keepdims=True)
        largest = most if largest is None else jnp.maximum(largest, most)
        for n in range(2):
            for a in range(SIDE):
                part[a * SIDE + 2 * half + n] = sums[
                    a * PART : a * PART + PART, n * 128 : n * 128 + 128
                ]
    factor = scale_for(jnp.max(largest, axis=1, keepdims=True))
    for n in range(SIDE * SIDE):
        codes[n, :PART, :] = encode(part[n], factor.astype(F32))
        codes[n, PART:, :] = jnp.broadcast_to(factor, (8, 128))
    for n, (a, b) in enumerate(OTHERS):
        peer = plane_at(a, b)
        send(
            codes.at[peer["lat"] * SIDE + peer["lon"]],
            got.at[n],
            rs_send.at[n],
            rs_recv.at[n],
            peer,
        )

    fetches[2].wait()
    prod[...] = jnp.dot(
        wts[...].reshape(TAPS * CH, FILT),
        gath[...].reshape(FILT, CELLS),
        preferred_element_type=F32,
    )
    sums = shifted_sums(lambda tap: prod[tap * CH : tap * CH + CH, :], places)
    mine = sums[0, 0]
    lat_out[0] = sums[1, 0][:, 0:256]
    lat_out[1] = sums[-1, 0][:, CELLS - 256 : CELLS]
    columns = [(a, b) for a in (-1, 0, 1) for b in (-1, 1)]
    for n, at in enumerate(columns):
        pt_out[n] = pack_column(sums[at])
    prod[0:CH, :] = mine
    for n, a in enumerate((1, -1)):
        send(lat_out.at[n], lat_in.at[n], ph_send.at[n], ph_recv.at[n], plane_at(a, 0))
    for n, (a, b) in enumerate(columns):
        send(pt_out.at[n], pt_in.at[n], ph_send.at[2 + n], ph_recv.at[2 + n], plane_at(a, b))

    mine_at = lat * SIDE + lon
    share = part[mine_at]
    for n, (a, b) in enumerate(OTHERS):
        arrived(got.at[n], rs_send.at[n], rs_recv.at[n], plane_at(-a, -b))
        share += decode(got[n])
    share *= scale
    factor = scale_for(jnp.max(jnp.max(jnp.abs(share), axis=0, keepdims=True), axis=1, keepdims=True))
    full[mine_at, :PART, :] = encode(share, factor.astype(F32))
    full[mine_at, PART:, :] = jnp.broadcast_to(factor, (8, 128))
    for n, (a, b) in enumerate(OTHERS):
        send(
            full.at[mine_at], full.at[mine_at], ag_send.at[n], ag_recv.at[n], plane_at(a, b)
        )

    for n, a in enumerate((1, -1)):
        arrived(lat_in.at[n], ph_send.at[n], ph_recv.at[n], plane_at(-a, 0))
    for n, (a, b) in enumerate(columns):
        arrived(pt_in.at[n], ph_send.at[2 + n], ph_recv.at[2 + n], plane_at(-a, -b))
    total = prod[0:CH, :]
    total += jnp.concatenate(
        [lat_in[0] * south, jnp.zeros((CH, CELLS - 512), F32), lat_in[1] * north], axis=1
    )
    for n, (a, b) in enumerate(columns):
        packed = pt_in[n]
        if a != 0:
            packed = packed * (south if a == 1 else north)
        total += unpack_column(packed, places, 0 if b == 1 else COLS - 1)
    xg_ref[...] = from_lanes(total.astype(BF16), spread, keep)

    def put(at_lat, at_lon):
        lanes = pl.ds(pl.multiple_of(at_lon * 128, 128), 128)
        wg_ref[pl.ds(at_lat * PER, PER), :, lanes] = decode(full[at_lat * SIDE + at_lon]).reshape(
            PER, CH, 128
        )

    put(lat, lon)
    for n, (a, b) in enumerate(OTHERS):
        peer = plane_at(-a, -b)
        arrived(
            full.at[peer["lat"] * SIDE + peer["lon"]], ag_send.at[n], ag_recv.at[n], peer
        )
        put(peer["lat"], peer["lon"])
    for copy in sends:
        copy.wait_send()


def body(inputs, weights, out_grad):
    nz = lax.axis_size("ch") // 2
    cells = CELLS * lax.axis_size("lat") * lax.axis_size("lon")
    dma = pltpu.SemaphoreType.DMA
    vmem = pl.BlockSpec(memory_space=pltpu.VMEM)
    whole = pl.BlockSpec(memory_space=pl.ANY)
    input_grad, weight_grad = pl.pallas_call(
        lambda *refs: kernel(nz, 1.0 / math.sqrt(cells), *refs),
        out_shape=(
            jax.ShapeDtypeStruct((CH * GROUPS, COLS), BF16),
            jax.ShapeDtypeStruct((SIDE * PER, CH, FILT), F32),
        ),
        in_specs=[whole] * 3,
        out_specs=(vmem, vmem),
        scratch_shapes=[
            pltpu.VMEM((CH * GROUPS, COLS), BF16),
            pltpu.VMEM((CH * GROUPS, COLS), BF16),
            pltpu.VMEM((9, CH, CELLS), BF16),
            pltpu.VMEM((SIDE * PART, CELLS), BF16),
            pltpu.VMEM((2 * nz, CH, CELLS), BF16),
            pltpu.VMEM((TAPS, CH, FILT), BF16),
            pltpu.VMEM((TAPS * CH, CELLS), F32),
            pltpu.VMEM((SIDE * SIDE, PART, 128), F32),
            pltpu.VMEM((SIDE * SIDE, PART + 8, 128), BF16),
            pltpu.VMEM((15, PART + 8, 128), BF16),
            pltpu.VMEM((SIDE * SIDE, PART + 8, 128), BF16),
            pltpu.VMEM((2, CH, 256), F32),
            pltpu.VMEM((2, CH, 256), F32),
            pltpu.VMEM((6, CH, 128), F32),
            pltpu.VMEM((6, CH, 128), F32),
            dma((3,)),
            dma((16,)),
            dma((16,)),
            dma((16,)),
            dma((16,)),
            dma((8,)),
            dma((8,)),
            dma((8,)),
            dma((8,)),
            dma((15,)),
            dma((15,)),
            dma((15,)),
            dma((15,)),
        ],
        compiler_params=pltpu.CompilerParams(
            collective_id=0, has_side_effects=True, vmem_limit_bytes=VMEM_BYTES
        ),
    )(
        inputs.reshape(CH * GROUPS, COLS),
        jnp.transpose(weights, (1, 0, 2)),
        out_grad.reshape(CH * GROUPS, COLS),
    )
    return input_grad.reshape(inputs.shape), jnp.transpose(weight_grad[:TAPS], (1, 0, 2))


def solution(mesh):
    in_specs = (P("ch", None, "lat", "lon"), P("ch", None, None), P("ch", None, "lat", "lon"))
    out_specs = (P("ch", None, "lat", "lon"), P("ch", None, None))
    return jax.shard_map(body, mesh=mesh, in_specs=in_specs, out_specs=out_specs, check_vma=False)
```

time: 68.4 us -> 51.7 us (0.76)
  Pallas kernels: 63.1 us -> 48.1 us
  local copies, waits for them, and re-layouts: 4.23 us -> 2.84 us
    pallas_call x1, Pallas kernels: 63.1 us -> 48.1 us  [body(): pl.pallas_call(lambda *refs: kernel(nz, 1.0 / math.sqrt(cells), *refs), o...]
    unnamed x8 -> x3, local copies, waits for them, and re-layouts: 4.23 us -> 0.63 us
    transpose x0 -> x1, local copies, waits for them, and re-layouts: none -> 2.21 us  [body(): jnp.transpose(weight_grad[:TAPS], (1, 0, 2))]
where the time goes in v2:
time: 51.7 us; the launch traced here: 51.5 us
  Pallas kernels  48.1 us (93%)
  local copies, waits for them, and re-layouts  2.84 us (5%)
  between operations  0.65 us (1%)
    pallas_call x1, Pallas kernels, body(): pl.pallas_call(lambda *refs: kernel(nz, 1.0 / math.sqrt(cells), *refs), o...  48.1 us
    transpose x1, local copies, waits for them, and re-layouts, body(): jnp.transpose(weight_grad[:TAPS], (1, 0, 2))  2.21 us

profile of v2, /device:TPU:1, one launch (start us, length us, event | category | flops | bytes accessed | tf_op | source)
XLA Modules:
  0.0 51.5 jit_solution(4141528667695235400)
XLA Ops:
  0.6 48.1 %shard_map.50 = (bf16[256,48]{1,0:T(8,128)(2,1)}, f32[28,16,512]{2,1,0:T(8,128)}) custom-call(bf16[256,48]{1,0:T(8,128)(2,1)} %bitcast.7, bf16[27,16,512]{2,1,0:T(8,128)(2,1)} %bitcast.6, bf16[256,48]{1,0:T(8,128)(2,1)} %bitcast.8), custom_call_target="tpu_custom_call" | custom-call | tf_op jit(solution)/shard_map/pallas_call | solution.py:448
  48.7 0.0 copy-start
  48.7 2.2 %slice_bitcast_fusion = f32[16,27,512]{2,0,1:T(8,128)} fusion(f32[28,16,512]{2,1,0:T(8,128)} %get-tuple-element.5), kind=kLoop, calls=%fused_computation | loop fusion | bytes 1769472 | tf_op jit(solution)/shard_map/transpose | solution.py:494
  50.9 0.0 copy-done
  50.9 0.6 %copy.6 = bf16[16,4,4,48]{3,2,1,0:T(4,128)(2,1)} copy(bf16[16,4,4,48]{3,2,1,0:T(4,128)(2,1)S(1)} %bitcast.9) | data formatting | bytes 49152
Async XLA Ops:
  48.7 2.2 %copy-start = (bf16[256,48]{1,0:T(8,128)(2,1)S(1)}, bf16[256,48]{1,0:T(8,128)(2,1)}, u32[]{:S(2)}) copy-start(bf16[256,48]{1,0:T(8,128)(2,1)} %get-tuple-element.4) | copy-start | bytes 73732

commit v3 on v2

--- a/solution.py
+++ b/solution.py
@@ -20,12 +20,12 @@
 SIDE = 4
 TAPS = 27
 PER = 7
-PART = PER * CH
+PART = PER * CH // 2
 FILT = 512
 STEP_LAT = LEV * COLS
 TOP = 2.0**30
 TINY = 1e-28
-VMEM_BYTES = 60 << 20
+VMEM_BYTES = 24 << 20
 OTHERS = sorted(
     ((a, b) for a in range(SIDE) for b in range(SIDE) if (a, b) != (0, 0)),
     key=lambda at: -(min(at[0], SIDE - at[0]) + min(at[1], SIDE - at[1])),
@@ -327,52 +327,105 @@
         )
     build(0)
     block_here(4, 4)
-    for hop in (3, 2, 1, -1):
+    for hop in (1, -1, 3, 2):
         to_chip(4 + hop, hop)
     block_here(-4, -4)
-    for hop in (-3, -2, -1, 1):
+    for hop in (-1, 1, -3, -2):
         to_chip(-4 + hop, hop)
     way = 4 - 8 * core
     far = z_at(-way)
     send(gath.at[far], gath.at[far], z_send.at[15], z_recv.at[15], {"ch": z_at(way)})
     build(1)
     build(-1)
-    for dist, hop in ((2, 1), (-2, -1), (3, -1), (-3, 1), (5, 1), (-5, -1), (6, 2), (-6, -2)):
+    near_tile = (z + 2) // 4 + 3
+
+    def tile_of(half, n):
+        return lax.rem(near_tile + 2 * half + n, 4)
+
+    def spread_out(half):
+        largest = None
+        for n in range(2):
+            filters = gath[pl.ds(tile_of(half, n) * 8, 8)].reshape(128, CELLS)
+            sums = lax.dot_general(
+                cols[...], filters, (((1,), (1,)), ((), ())), preferred_element_type=F32
+            )
+            most = jnp.max(jnp.abs(sums), axis=0, keepdims=True)
+            largest = most if largest is None else jnp.maximum(largest, most)
+            for a in range(SIDE):
+                for side in range(2):
+                    at = (2 * a + side) * PART
+                    part[half, a * SIDE + 2 * n + side] = sums[at : at + PART]
+        factor = scale_for(jnp.max(largest, axis=1, keepdims=True))
+        for n in range(SIDE * SIDE):
+            codes[half, n, :PART, :] = encode(part[half, n], factor.astype(F32))
+            codes[half, n, PART:, :] = jnp.broadcast_to(factor, (8, 128))
+        for n, (a, b) in enumerate(OTHERS):
+            peer = plane_at(a, b)
+            send(
+                codes.at[half, peer["lat"] * SIDE + peer["lon"]],
+                got.at[half, n],
+                rs_send.at[half, n],
+                rs_recv.at[half, n],
+                peer,
+            )
+
+    mine_at = lat * SIDE + lon
+
+    def add_up(half):
+        share = part[half, mine_at]
+        for n, (a, b) in enumerate(OTHERS):
+            arrived(got.at[half, n], rs_send.at[half, n], rs_recv.at[half, n], plane_at(-a, -b))
+            share += decode(got[half, n])
+        share *= scale
+        largest = jnp.max(jnp.max(jnp.abs(share), axis=0, keepdims=True), axis=1, keepdims=True)
+        factor = scale_for(largest)
+        full[half, mine_at, :PART, :] = encode(share, factor.astype(F32))
+        full[half, mine_at, PART:, :] = jnp.broadcast_to(factor, (8, 128))
+        for n, (a, b) in enumerate(OTHERS):
+            send(
+                full.at[half, mine_at],
+                full.at[half, mine_at],
+                ag_send.at[half, n],
+                ag_recv.at[half, n],
+                plane_at(a, b),
+            )
+
+    def put(half, at_lat, at_lon):
+        lanes = pl.ds(pl.multiple_of(tile_of(half, at_lon // 2) * 128, 128), 128)
+        row = at_lat * 2 * PER + (at_lon % 2) * PER
+        value = decode(full[half, at_lat * SIDE + at_lon]).reshape(PER, 8, 128)
+        for n in (6, 5):
+            wg_ref[pl.ds(jnp.minimum(row + n, TAPS * 2 - 1), 1), :, lanes] = value[n : n + 1]
+        wg_ref[pl.ds(row, 5), :, lanes] = value[:5]
+
+    def collect(half):
+        put(half, lat, lon)
+        for n, (a, b) in enumerate(OTHERS):
+            peer = plane_at(-a, -b)
+            arrived(
+                full.at[half, peer["lat"] * SIDE + peer["lon"]],
+                ag_send.at[half, n],
+                ag_recv.at[half, n],
+                peer,
+            )
+            put(half, peer["lat"], peer["lon"])
+
+    def sibling_here(dists):
+        for dist in dists:
+            slot = lax.rem(z - dist + nz, nz) * 2 + (1 - core)
+            at = (dist + 7) % 16
+            arrived(gath.at[slot], sib_send.at[at], sib_recv.at[at], {"ch": sibling})
+
+    for dist, hop in ((2, 1), (-2, -1), (3, -1), (-3, 1), (5, 1), (-5, -1)):
         block_here(dist, hop)
-    for dist, hop in ((7, 3), (-7, -3)):
+    sibling_here((0, 1, -1, 4, -4, 2, -2, 3, -3, 5, -5))
+    spread_out(0)
+    for dist, hop in ((6, 2), (-6, -2), (7, 3), (-7, -3)):
         block_here(dist, hop)
     block_here(8, way)
-    for dist in (0, 1, -1, 4, -4, 2, -2, 3, -3, 5, -5, 6, -6, 7, -7, 8):
-        slot = lax.rem(z - dist + nz, nz) * 2 + (1 - core)
-        at = (dist + 7) % 16
-        arrived(gath.at[slot], sib_send.at[at], sib_recv.at[at], {"ch": sibling})
-
-    largest = None
-    for half in range(2):
-        filters = gath[half * 16 : half * 16 + 16].reshape(FILT // 2, CELLS)
-        sums = lax.dot_general(
-            cols[...], filters, (((1,), (1,)), ((), ())), preferred_element_type=F32
-        )
-        most = jnp.max(jnp.abs(sums), axis=0, keepdims=True)
-        largest = most if largest is None else jnp.maximum(largest, most)
-        for n in range(2):
-            for a in range(SIDE):
-                part[a * SIDE + 2 * half + n] = sums[
-                    a * PART : a * PART + PART, n * 128 : n * 128 + 128
-                ]
-    factor = scale_for(jnp.max(largest, axis=1, keepdims=True))
-    for n in range(SIDE * SIDE):
-        codes[n, :PART, :] = encode(part[n], factor.astype(F32))
-        codes[n, PART:, :] = jnp.broadcast_to(factor, (8, 128))
-    for n, (a, b) in enumerate(OTHERS):
-        peer = plane_at(a, b)
-        send(
-            codes.at[peer["lat"] * SIDE + peer["lon"]],
-            got.at[n],
-            rs_send.at[n],
-            rs_recv.at[n],
-            peer,
-        )
+    sibling_here((6, -6, 7, -7, 8))
+    spread_out(1)
+    add_up(0)
 
     fetches[2].wait()
     prod[...] = jnp.dot(
@@ -393,19 +446,7 @@
     for n, (a, b) in enumerate(columns):
         send(pt_out.at[n], pt_in.at[n], ph_send.at[2 + n], ph_recv.at[2 + n], plane_at(a, b))
 
-    mine_at = lat * SIDE + lon
-    share = part[mine_at]
-    for n, (a, b) in enumerate(OTHERS):
-        arrived(got.at[n], rs_send.at[n], rs_recv.at[n], plane_at(-a, -b))
-        share += decode(got[n])
-    share *= scale
-    factor = scale_for(jnp.max(jnp.max(jnp.abs(share), axis=0, keepdims=True), axis=1, keepdims=True))
-    full[mine_at, :PART, :] = encode(share, factor.astype(F32))
-    full[mine_at, PART:, :] = jnp.broadcast_to(factor, (8, 128))
-    for n, (a, b) in enumerate(OTHERS):
-        send(
-            full.at[mine_at], full.at[mine_at], ag_send.at[n], ag_recv.at[n], plane_at(a, b)
-        )
+    add_up(1)
 
     for n, a in enumerate((1, -1)):
         arrived(lat_in.at[n], ph_send.at[n], ph_recv.at[n], plane_at(-a, 0))
@@ -422,19 +463,8 @@
         total += unpack_column(packed, places, 0 if b == 1 else COLS - 1)
     xg_ref[...] = from_lanes(total.astype(BF16), spread, keep)
 
-    def put(at_lat, at_lon):
-        lanes = pl.ds(pl.multiple_of(at_lon * 128, 128), 128)
-        wg_ref[pl.ds(at_lat * PER, PER), :, lanes] = decode(full[at_lat * SIDE + at_lon]).reshape(
-            PER, CH, 128
-        )
-
-    put(lat, lon)
-    for n, (a, b) in enumerate(OTHERS):
-        peer = plane_at(-a, -b)
-        arrived(
-            full.at[peer["lat"] * SIDE + peer["lon"]], ag_send.at[n], ag_recv.at[n], peer
-        )
-        put(peer["lat"], peer["lon"])
+    collect(0)
+    collect(1)
     for copy in sends:
         copy.wait_send()
 
@@ -444,12 +474,12 @@
     cells = CELLS * lax.axis_size("lat") * lax.axis_size("lon")
     dma = pltpu.SemaphoreType.DMA
     vmem = pl.BlockSpec(memory_space=pltpu.VMEM)
-    whole = pl.BlockSpec(memory_space=pl.ANY)
+    whole = pl.BlockSpec(memory_space=pltpu.HBM)
     input_grad, weight_grad = pl.pallas_call(
         lambda *refs: kernel(nz, 1.0 / math.sqrt(cells), *refs),
         out_shape=(
             jax.ShapeDtypeStruct((CH * GROUPS, COLS), BF16),
-            jax.ShapeDtypeStruct((SIDE * PER, CH, FILT), F32),
+            jax.ShapeDtypeStruct((TAPS * 2, 8, FILT), F32),
         ),
         in_specs=[whole] * 3,
         out_specs=(vmem, vmem),
@@ -457,14 +487,14 @@
             pltpu.VMEM((CH * GROUPS, COLS), BF16),
             pltpu.VMEM((CH * GROUPS, COLS), BF16),
             pltpu.VMEM((9, CH, CELLS), BF16),
-            pltpu.VMEM((SIDE * PART, CELLS), BF16),
+            pltpu.VMEM((2 * SIDE * PART, CELLS), BF16),
             pltpu.VMEM((2 * nz, CH, CELLS), BF16),
             pltpu.VMEM((TAPS, CH, FILT), BF16),
             pltpu.VMEM((TAPS * CH, CELLS), F32),
-            pltpu.VMEM((SIDE * SIDE, PART, 128), F32),
-            pltpu.VMEM((SIDE * SIDE, PART + 8, 128), BF16),
-            pltpu.VMEM((15, PART + 8, 128), BF16),
-            pltpu.VMEM((SIDE * SIDE, PART + 8, 128), BF16),
+            pltpu.VMEM((2, SIDE * SIDE, PART, 128), F32),
+            pltpu.VMEM((2, SIDE * SIDE, PART + 8, 128), BF16),
+            pltpu.VMEM((2, 15, PART + 8, 128), BF16),
+            pltpu.VMEM((2, SIDE * SIDE, PART + 8, 128), BF16),
             pltpu.VMEM((2, CH, 256), F32),
             pltpu.VMEM((2, CH, 256), F32),
             pltpu.VMEM((6, CH, 128), F32),
@@ -478,20 +508,26 @@
             dma((8,)),
             dma((8,)),
             dma((8,)),
-            dma((15,)),
-            dma((15,)),
-            dma((15,)),
-            dma((15,)),
+            dma((2, 15)),
+            dma((2, 15)),
+            dma((2, 15)),
+            dma((2, 15)),
         ],
         compiler_params=pltpu.CompilerParams(
             collective_id=0, has_side_effects=True, vmem_limit_bytes=VMEM_BYTES
         ),
     )(
-        inputs.reshape(CH * GROUPS, COLS),
-        jnp.transpose(weights, (1, 0, 2)),
-        out_grad.reshape(CH * GROUPS, COLS),
+        *(
+            pltpu.with_memory_space_constraint(array, pltpu.HBM)
+            for array in (
+                inputs.reshape(CH * GROUPS, COLS),
+                jnp.transpose(weights, (1, 0, 2)),
+                out_grad.reshape(CH * GROUPS, COLS),
+            )
+        )
     )
-    return input_grad.reshape(inputs.shape), jnp.transpose(weight_grad[:TAPS], (1, 0, 2))
+    weight_grad = weight_grad.reshape(TAPS, CH, FILT)
+    return input_grad.reshape(inputs.shape), jnp.transpose(weight_grad, (1, 0, 2))
 
 
 def solution(mesh):

time: 51.7 us -> 47.1 us (0.911)
  Pallas kernels: 48.1 us -> 44.7 us
  local copies, waits for them, and re-layouts: 2.84 us -> 1.54 us
    pallas_call x1, Pallas kernels: 48.1 us -> 44.7 us  [body(): pl.pallas_call(lambda *refs: kernel(nz, 1.0 / math.sqrt(cells), *refs), o...]
    transpose x1 -> x0, local copies, waits for them, and re-layouts: 2.21 us -> none  [body(): jnp.transpose(weight_grad[:TAPS], (1, 0, 2))]
    unnamed x3 -> x2, local copies, waits for them, and re-layouts: 0.63 us -> 1.54 us
where the time goes in v3:
time: 47.1 us; the launch traced here: 46.9 us
  Pallas kernels  44.7 us (95%)
  local copies, waits for them, and re-layouts  1.54 us (3%)
  between operations  0.64 us (1%)
    pallas_call x1, Pallas kernels, body(): pl.pallas_call(lambda *refs: kernel(nz, 1.0 / math.sqrt(cells), *refs), o...  44.7 us
    unnamed x2, local copies, waits for them, and re-layouts  1.54 us

profile of v3, /device:TPU:1, one launch (start us, length us, event | category | flops | bytes accessed | tf_op | source)
XLA Modules:
  0.0 46.9 jit_solution(16420692284020941863)
XLA Ops:
  0.6 44.7 %shard_map.50 = (bf16[256,48]{1,0:T(8,128)(2,1)S(1)}, f32[54,8,512]{2,1,0:T(8,128)S(1)}) custom-call(bf16[256,48]{1,0:T(8,128)(2,1)} %bitcast.10, bf16[27,16,512]{2,1,0:T(8,128)(2,1)} %bitcast.9, bf16[256,48]{1,0:T(8,128)(2,1)} %bitcast.11), custom_call_target="tpu_custom_call" | custom-call | tf_op jit(solution)/shard_map/pallas_call | solution.py:478
  45.4 0.6 %copy.7 = bf16[16,4,4,48]{3,2,1,0:T(4,128)(2,1)} copy(bf16[16,4,4,48]{3,2,1,0:T(4,128)(2,1)S(1)} %bitcast.8) | data formatting | bytes 49152
  46.0 0.9 %copy.8 = f32[16,27,512]{2,0,1:T(8,128)} copy(f32[16,27,512]{2,0,1:T(8,128)S(1)} %bitcast.7) | data formatting | bytes 1769472

commit v4 on v3

--- a/solution.py
+++ b/solution.py
@@ -30,6 +30,8 @@
     ((a, b) for a in range(SIDE) for b in range(SIDE) if (a, b) != (0, 0)),
     key=lambda at: -(min(at[0], SIDE - at[0]) + min(at[1], SIDE - at[1])),
 )
+PIECES = (((0, PART + 8),), ((0, PART + 8),))
+ORDER = [(half, piece) for half in range(2) for piece in range(len(PIECES[half]))]
 NEAR = [(a, b) for a in (-1, 0, 1) for b in (-1, 0, 1) if (a, b) != (0, 0)]
 
 
@@ -158,11 +160,10 @@
     return (square * scaled * jnp.abs(scaled)).astype(BF16)
 
 
-def decode(codes):
-    inverse = 1.0 / codes[PART:, :].astype(F32)
-    power = codes[:PART, :].astype(F32).reshape(PART // 8, 8, 128)
+def decode(codes, inverse):
+    power = codes.astype(F32).reshape(codes.shape[0] // 8, 8, 128)
     root = lax.rsqrt(lax.rsqrt(jnp.abs(power))) * inverse[None]
-    return jnp.where(power < 0, -root, root).reshape(PART, 128)
+    return jnp.where(power < 0, -root, root).reshape(codes.shape)
 
 
 def scale_for(largest):
@@ -188,6 +189,8 @@
     codes,
     got,
     full,
+    scales,
+    least_of,
     lat_out,
     lat_in,
     pt_out,
@@ -242,14 +245,12 @@
     fetches[0].wait()
     gath[ch] = to_lanes(g_own[...], spread, keep)
     fetches[1].wait()
-    field[4] = to_lanes(x_own[...], spread, keep)
+    field[8] = to_lanes(x_own[...], spread, keep)
 
     pl.semaphore_wait(barrier, len(peers))
 
-    sends = []
-
-    def send(src, dst, send_sem, recv_sem, peer):
-        copy = pltpu.make_async_remote_copy(
+    def copy_of(src, dst, send_sem, recv_sem, peer):
+        return pltpu.make_async_remote_copy(
             src_ref=src,
             dst_ref=dst,
             send_sem=send_sem,
@@ -257,18 +258,15 @@
             device_id=peer,
             device_id_type=MESH,
         )
-        copy.start()
-        sends.append(copy)
-
-    def arrived(dst, send_sem, recv_sem, peer):
-        pltpu.make_async_remote_copy(
-            src_ref=dst,
-            dst_ref=dst,
-            send_sem=send_sem,
-            recv_sem=recv_sem,
-            device_id=peer,
-            device_id_type=MESH,
-        ).wait_recv()
+
+    def send(*args):
+        copy_of(*args).start()
+
+    def arrived(dst, sem):
+        copy_of(dst, dst, sem, sem, {"ch": sibling}).wait_recv()
+
+    def sent(src, sem):
+        copy_of(src, src, sem, sem, {"ch": sibling}).wait_send()
 
     def to_chip(dist, hop):
         slot = z_at(hop - dist)
@@ -276,39 +274,32 @@
         send(
             gath.at[slot],
             gath.at[slot],
-            z_send.at[at],
+            z_send,
             z_recv.at[at],
             {"ch": z_at(hop)},
         )
 
     def to_sibling(dist):
         slot = z_at(-dist)
-        at = (dist + 7) % 16
-        send(gath.at[slot], gath.at[slot], sib_send.at[at], sib_recv.at[at], {"ch": sibling})
-
-    def block_here(dist, hop):
-        at = (dist + 7) % 16
-        arrived(gath.at[z_at(-dist)], z_send.at[at], z_recv.at[at], {"ch": z_at(-hop)})
+        late = 0 if abs(dist) <= 5 else 1
+        send(gath.at[slot], gath.at[slot], sib_send, sib_recv.at[late], {"ch": sibling})
+
+    def block_here(dist):
+        arrived(gath.at[z_at(-dist)], z_recv.at[(dist + 7) % 16])
         to_sibling(dist)
 
     for dist in (4, -4, 1, -1):
         to_chip(dist, dist)
     to_sibling(0)
     for n, (a, b) in enumerate(NEAR):
-        send(
-            field.at[4],
-            field.at[(1 - a) * 3 + 1 - b],
-            xh_send.at[n],
-            xh_recv.at[n],
-            plane_at(a, b),
-        )
+        send(field.at[8], field.at[n], xh_send, xh_recv, plane_at(-a, -b))
 
     south = jnp.where(lat > 0, 1.0, 0.0).astype(F32)
     north = jnp.where(lat < SIDE - 1, 1.0, 0.0).astype(F32)
     inside = {-1: south, 1: north}
 
     def near(a, b):
-        block = field[(a + 1) * 3 + b + 1].astype(F32)
+        block = field[NEAR.index((a, b)) if (a, b) != (0, 0) else 8].astype(F32)
         return block if a == 0 else block * inside[a]
 
     def build(d_lat):
@@ -317,24 +308,21 @@
             cols[tap * CH : tap * CH + CH, :] = value.astype(BF16)
 
     cols[TAPS * CH :, :] = jnp.zeros((CH, CELLS), BF16)
-    block_here(1, 1)
+    block_here(1)
     to_chip(2, 1)
-    block_here(-1, -1)
+    block_here(-1)
     to_chip(-2, -1)
-    for n, (a, b) in enumerate(NEAR):
-        arrived(
-            field.at[(1 - a) * 3 + 1 - b], xh_send.at[n], xh_recv.at[n], plane_at(-a, -b)
-        )
+    arrived(field.at[pl.ds(0, 8)], xh_recv)
     build(0)
-    block_here(4, 4)
-    for hop in (1, -1, 3, 2):
+    block_here(4)
+    for hop in (3, 2, 1, -1):
         to_chip(4 + hop, hop)
-    block_here(-4, -4)
-    for hop in (-1, 1, -3, -2):
+    block_here(-4)
+    for hop in (-3, -2, -1, 1):
         to_chip(-4 + hop, hop)
     way = 4 - 8 * core
     far = z_at(-way)
-    send(gath.at[far], gath.at[far], z_send.at[15], z_recv.at[15], {"ch": z_at(way)})
+    send(gath.at[far], gath.at[far], z_send, z_recv.at[15], {"ch": z_at(way)})
     build(1)
     build(-1)
     near_tile = (z + 2) // 4 + 3
@@ -356,76 +344,88 @@
                     at = (2 * a + side) * PART
                     part[half, a * SIDE + 2 * n + side] = sums[at : at + PART]
         factor = scale_for(jnp.max(largest, axis=1, keepdims=True))
-        for n in range(SIDE * SIDE):
-            codes[half, n, :PART, :] = encode(part[half, n], factor.astype(F32))
-            codes[half, n, PART:, :] = jnp.broadcast_to(factor, (8, 128))
+        scales[half] = jnp.broadcast_to(factor, (8, 128)).astype(F32)
         for n, (a, b) in enumerate(OTHERS):
             peer = plane_at(a, b)
-            send(
-                codes.at[half, peer["lat"] * SIDE + peer["lon"]],
-                got.at[half, n],
-                rs_send.at[half, n],
-                rs_recv.at[half, n],
-                peer,
+            codes[half, n, :8, :] = jnp.broadcast_to(factor, (8, 128))
+            codes[half, n, 8:, :] = encode(
+                part[half, peer["lat"] * SIDE + peer["lon"]], factor.astype(F32)
             )
+        for piece, (start, end) in enumerate(PIECES[half]):
+            rows = pl.ds(start, end - start)
+            for n, (a, b) in enumerate(OTHERS):
+                send(
+                    codes.at[half, n, rows],
+                    got.at[half, n, rows],
+                    rs_send.at[half, piece],
+                    rs_recv.at[half, piece],
+                    plane_at(a, b),
+                )
 
     mine_at = lat * SIDE + lon
 
-    def add_up(half):
-        share = part[half, mine_at]
-        for n, (a, b) in enumerate(OTHERS):
-            arrived(got.at[half, n], rs_send.at[half, n], rs_recv.at[half, n], plane_at(-a, -b))
-            share += decode(got[half, n])
-        share *= scale
-        largest = jnp.max(jnp.max(jnp.abs(share), axis=0, keepdims=True), axis=1, keepdims=True)
-        factor = scale_for(largest)
-        full[half, mine_at, :PART, :] = encode(share, factor.astype(F32))
-        full[half, mine_at, PART:, :] = jnp.broadcast_to(factor, (8, 128))
+    def add_up(half, piece):
+        start, end = PIECES[half][piece]
+        rows = pl.ds(start, end - start)
+        arrived(got.at[half, pl.ds(0, 15), rows], rs_recv.at[half, piece])
+        if piece == 0:
+            least = scales[half]
+            for n in range(len(OTHERS)):
+                least = jnp.minimum(least, got[half, n, :8, :].astype(F32))
+            least_of[half] = least
+        low, high = max(start - 8, 0), end - 8
+        share = part[half, mine_at, low:high]
+        for n in range(len(OTHERS)):
+            share += decode(
+                got[half, n, low + 8 : high + 8, :], 1.0 / got[half, n, :8, :].astype(F32)
+            )
+        factor = least_of[half] * (1.0 / (SIDE * SIDE))
+        share = share.reshape((high - low) // 8, 8, 128)
+        full[half, 15, low:high, :] = encode(share, factor[None]).reshape(high - low, 128)
+        rows = pl.ds(low, high - low)
         for n, (a, b) in enumerate(OTHERS):
             send(
-                full.at[half, mine_at],
-                full.at[half, mine_at],
-                ag_send.at[half, n],
-                ag_recv.at[half, n],
+                full.at[half, 15, rows],
+                full.at[half, n, rows],
+                ag_send.at[half, piece],
+                ag_recv.at[half, piece],
                 plane_at(a, b),
             )
 
-    def put(half, at_lat, at_lon):
+    def put(half, piece, n, at_lat, at_lon, inverse):
+        start, end = PIECES[half][piece]
+        low, high = max(start // 8 - 1, 0), end // 8 - 1
         lanes = pl.ds(pl.multiple_of(tile_of(half, at_lon // 2) * 128, 128), 128)
         row = at_lat * 2 * PER + (at_lon % 2) * PER
-        value = decode(full[half, at_lat * SIDE + at_lon]).reshape(PER, 8, 128)
-        for n in (6, 5):
-            wg_ref[pl.ds(jnp.minimum(row + n, TAPS * 2 - 1), 1), :, lanes] = value[n : n + 1]
-        wg_ref[pl.ds(row, 5), :, lanes] = value[:5]
-
-    def collect(half):
-        put(half, lat, lon)
+        value = decode(full[half, n, low * 8 : high * 8, :], inverse)
+        value = value.reshape(high - low, 8, 128)
+        for k in range(high - 1, max(low, 5) - 1, -1):
+            at = jnp.minimum(row + k, TAPS * 2 - 1)
+            wg_ref[pl.ds(at, 1), :, lanes] = value[k - low : k - low + 1]
+        for k in range(low, min(high, 5)):
+            wg_ref[pl.ds(row + k, 1), :, lanes] = value[k - low : k - low + 1]
+
+    def collect(half, piece):
+        start, end = PIECES[half][piece]
+        low, high = max(start - 8, 0), end - 8
+        inverse = (SIDE * SIDE * scale) / least_of[half]
+        put(half, piece, 15, lat, lon, inverse)
+        arrived(full.at[half, pl.ds(0, 15), pl.ds(low, high - low)], ag_recv.at[half, piece])
         for n, (a, b) in enumerate(OTHERS):
             peer = plane_at(-a, -b)
-            arrived(
-                full.at[half, peer["lat"] * SIDE + peer["lon"]],
-                ag_send.at[half, n],
-                ag_recv.at[half, n],
-                peer,
-            )
-            put(half, peer["lat"], peer["lon"])
-
-    def sibling_here(dists):
-        for dist in dists:
-            slot = lax.rem(z - dist + nz, nz) * 2 + (1 - core)
-            at = (dist + 7) % 16
-            arrived(gath.at[slot], sib_send.at[at], sib_recv.at[at], {"ch": sibling})
-
-    for dist, hop in ((2, 1), (-2, -1), (3, -1), (-3, 1), (5, 1), (-5, -1)):
-        block_here(dist, hop)
-    sibling_here((0, 1, -1, 4, -4, 2, -2, 3, -3, 5, -5))
+            put(half, piece, n, peer["lat"], peer["lon"], inverse)
+
+    for dist in (2, -2, 3, -3, 5, -5):
+        block_here(dist)
+    arrived(gath.at[pl.ds(0, 11)], sib_recv.at[0])
     spread_out(0)
-    for dist, hop in ((6, 2), (-6, -2), (7, 3), (-7, -3)):
-        block_here(dist, hop)
-    block_here(8, way)
-    sibling_here((6, -6, 7, -7, 8))
+    for dist in (6, -6, 7, -7, 8):
+        block_here(dist)
+    arrived(gath.at[pl.ds(0, 5)], sib_recv.at[1])
     spread_out(1)
-    add_up(0)
+    sent(field.at[pl.ds(0, 8)], xh_send)
+    sent(gath.at[pl.ds(0, 15)], z_send)
+    sent(gath.at[pl.ds(0, 16)], sib_send)
 
     fetches[2].wait()
     prod[...] = jnp.dot(
@@ -442,16 +442,15 @@
         pt_out[n] = pack_column(sums[at])
     prod[0:CH, :] = mine
     for n, a in enumerate((1, -1)):
-        send(lat_out.at[n], lat_in.at[n], ph_send.at[n], ph_recv.at[n], plane_at(a, 0))
+        send(lat_out.at[n], lat_in.at[n], ph_send.at[0], ph_recv.at[0], plane_at(a, 0))
     for n, (a, b) in enumerate(columns):
-        send(pt_out.at[n], pt_in.at[n], ph_send.at[2 + n], ph_recv.at[2 + n], plane_at(a, b))
-
-    add_up(1)
-
-    for n, a in enumerate((1, -1)):
-        arrived(lat_in.at[n], ph_send.at[n], ph_recv.at[n], plane_at(-a, 0))
-    for n, (a, b) in enumerate(columns):
-        arrived(pt_in.at[n], ph_send.at[2 + n], ph_recv.at[2 + n], plane_at(-a, -b))
+        send(pt_out.at[n], pt_in.at[n], ph_send.at[1], ph_recv.at[1], plane_at(a, b))
+
+    for half, piece in ORDER:
+        add_up(half, piece)
+
+    arrived(lat_in, ph_recv.at[0])
+    arrived(pt_in, ph_recv.at[1])
     total = prod[0:CH, :]
     total += jnp.concatenate(
         [lat_in[0] * south, jnp.zeros((CH, CELLS - 512), F32), lat_in[1] * north], axis=1
@@ -463,10 +462,17 @@
         total += unpack_column(packed, places, 0 if b == 1 else COLS - 1)
     xg_ref[...] = from_lanes(total.astype(BF16), spread, keep)
 
-    collect(0)
-    collect(1)
-    for copy in sends:
-        copy.wait_send()
+    sent(lat_out, ph_send.at[0])
+    sent(pt_out, ph_send.at[1])
+    for half, piece in ORDER:
+        start, end = PIECES[half][piece]
+        sent(codes.at[half, pl.ds(0, 15), pl.ds(start, end - start)], rs_send.at[half, piece])
+    for half, piece in ORDER:
+        collect(half, piece)
+    for half, piece in ORDER:
+        start, end = PIECES[half][piece]
+        low, high = max(start - 8, 0), end - 8
+        sent(full.at[half, pl.ds(0, 15), pl.ds(low, high - low)], ag_send.at[half, piece])
 
 
 def body(inputs, weights, out_grad):
@@ -492,26 +498,28 @@
             pltpu.VMEM((TAPS, CH, FILT), BF16),
             pltpu.VMEM((TAPS * CH, CELLS), F32),
             pltpu.VMEM((2, SIDE * SIDE, PART, 128), F32),
-            pltpu.VMEM((2, SIDE * SIDE, PART + 8, 128), BF16),
             pltpu.VMEM((2, 15, PART + 8, 128), BF16),
-            pltpu.VMEM((2, SIDE * SIDE, PART + 8, 128), BF16),
+            pltpu.VMEM((2, 15, PART + 8, 128), BF16),
+            pltpu.VMEM((2, SIDE * SIDE, PART, 128), BF16),
+            pltpu.VMEM((2, 8, 128), F32),
+            pltpu.VMEM((2, 8, 128), F32),
             pltpu.VMEM((2, CH, 256), F32),
             pltpu.VMEM((2, CH, 256), F32),
             pltpu.VMEM((6, CH, 128), F32),
             pltpu.VMEM((6, CH, 128), F32),
             dma((3,)),
+            dma,
             dma((16,)),
-            dma((16,)),
-            dma((16,)),
-            dma((16,)),
-            dma((8,)),
-            dma((8,)),
-            dma((8,)),
-            dma((8,)),
-            dma((2, 15)),
-            dma((2, 15)),
-            dma((2, 15)),
-            dma((2, 15)),
+            dma,
+            dma((2,)),
+            dma,
+            dma,
+            dma((2,)),
+            dma((2,)),
+            dma((2, 2)),
+            dma((2, 2)),
+            dma((2, 2)),
+            dma((2, 2)),
         ],
         compiler_params=pltpu.CompilerParams(
             collective_id=0, has_side_effects=True, vmem_limit_bytes=VMEM_BYTES

time: 47.1 us -> 44 us (0.934)
  Pallas kernels: 44.7 us -> 41.7 us
    pallas_call x1, Pallas kernels: 44.7 us -> 41.7 us  [body(): pl.pallas_call(lambda *refs: kernel(nz, 1.0 / math.sqrt(cells), *refs), o...]
where the time goes in v4:
time: 44 us; the launch traced here: 43.9 us
  Pallas kernels  41.7 us (95%)
  local copies, waits for them, and re-layouts  1.54 us (4%)
  between operations  0.64 us (1%)
    pallas_call x1, Pallas kernels, body(): pl.pallas_call(lambda *refs: kernel(nz, 1.0 / math.sqrt(cells), *refs), o...  41.7 us
    unnamed x2, local copies, waits for them, and re-layouts  1.54 us

profile of v4, /device:TPU:1, one launch (start us, length us, event | category | flops | bytes accessed | tf_op | source)
XLA Modules:
  0.0 43.9 jit_solution(16662378024257756779)
XLA Ops:
  0.6 41.7 %shard_map.50 = (bf16[256,48]{1,0:T(8,128)(2,1)S(1)}, f32[54,8,512]{2,1,0:T(8,128)S(1)}) custom-call(bf16[256,48]{1,0:T(8,128)(2,1)} %bitcast.10, bf16[27,16,512]{2,1,0:T(8,128)(2,1)} %bitcast.9, bf16[256,48]{1,0:T(8,128)(2,1)} %bitcast.11), custom_call_target="tpu_custom_call" | custom-call | tf_op jit(solution)/shard_map/pallas_call | solution.py:484
  42.3 0.6 %copy.7 = bf16[16,4,4,48]{3,2,1,0:T(4,128)(2,1)} copy(bf16[16,4,4,48]{3,2,1,0:T(4,128)(2,1)S(1)} %bitcast.8) | data formatting | bytes 49152
  42.9 0.9 %copy.8 = f32[16,27,512]{2,0,1:T(8,128)} copy(f32[16,27,512]{2,0,1:T(8,128)S(1)} %bitcast.7) | data formatting | bytes 1769472

commit v5 on v4

--- a/solution.py
+++ b/solution.py
@@ -315,10 +315,10 @@
     arrived(field.at[pl.ds(0, 8)], xh_recv)
     build(0)
     block_here(4)
-    for hop in (3, 2, 1, -1):
+    for hop in (3, 1, 2, -1):
         to_chip(4 + hop, hop)
     block_here(-4)
-    for hop in (-3, -2, -1, 1):
+    for hop in (-3, -1, -2, 1):
         to_chip(-4 + hop, hop)
     way = 4 - 8 * core
     far = z_at(-way)
@@ -473,6 +473,17 @@
         start, end = PIECES[half][piece]
         low, high = max(start - 8, 0), end - 8
         sent(full.at[half, pl.ds(0, 15), pl.ds(low, high - low)], ag_send.at[half, piece])
+
+
+def keep_both(x_ref, w_ref, x_out, w_out, sems):
+    copies = [
+        pltpu.make_async_copy(w_ref, w_out, sems.at[0]),
+        pltpu.make_async_copy(x_ref, x_out, sems.at[1]),
+    ]
+    for copy in copies:
+        copy.start()
+    for copy in copies:
+        copy.wait()
 
 
 def body(inputs, weights, out_grad):
@@ -534,6 +545,17 @@
             )
         )
     )
+    input_grad, weight_grad = pl.pallas_call(
+        keep_both,
+        out_shape=(
+            jax.ShapeDtypeStruct((CH * GROUPS, COLS), BF16),
+            jax.ShapeDtypeStruct((TAPS * 2, 8, FILT), F32),
+        ),
+        in_specs=[vmem, vmem],
+        out_specs=[pl.BlockSpec(memory_space=pl.ANY)] * 2,
+        scratch_shapes=[dma((2,))],
+        compiler_params=pltpu.CompilerParams(vmem_limit_bytes=4 << 20),
+    )(input_grad, weight_grad)
     weight_grad = weight_grad.reshape(TAPS, CH, FILT)
     return input_grad.reshape(inputs.shape), jnp.transpose(weight_grad, (1, 0, 2))
 

time: 44 us -> 42.6 us (0.968)
  local copies, waits for them, and re-layouts: 1.54 us -> 0 us
    unnamed x2 -> x0, local copies, waits for them, and re-layouts: 1.54 us -> none
    pallas_call x0 -> x1, Pallas kernels: none -> 0.94 us  [body(): pl.pallas_call(keep_both, out_shape=(jax.ShapeDtypeStruct((CH * GROUPS, C...]
    pallas_call x1, Pallas kernels: 41.7 us -> 40.9 us  [body(): pl.pallas_call(lambda *refs: kernel(nz, 1.0 / math.sqrt(cells), *refs), o...]
where the time goes in v5:
time: 42.6 us; the launch traced here: 42.5 us
  Pallas kernels  41.9 us (98%)
  between operations  0.64 us (2%)
    pallas_call x1, Pallas kernels, body(): pl.pallas_call(lambda *refs: kernel(nz, 1.0 / math.sqrt(cells), *refs), o...  40.9 us
    pallas_call x1, Pallas kernels, body(): pl.pallas_call(keep_both, out_shape=(jax.ShapeDtypeStruct((CH * GROUPS, C...  0.94 us

profile of v5, /device:TPU:1, one launch (start us, length us, event | category | flops | bytes accessed | tf_op | source)
XLA Modules:
  0.0 42.5 jit_solution(10166085315837054898)
XLA Ops:
  0.6 40.9 %shard_map.50 = (bf16[256,48]{1,0:T(8,128)(2,1)S(1)}, f32[54,8,512]{2,1,0:T(8,128)S(1)}) custom-call(bf16[256,48]{1,0:T(8,128)(2,1)} %bitcast.8, bf16[27,16,512]{2,1,0:T(8,128)(2,1)} %bitcast.7, bf16[256,48]{1,0:T(8,128)(2,1)} %bitcast.9), custom_call_target="tpu_custom_call" | custom-call | tf_op jit(solution)/shard_map/pallas_call | solution.py:495
  41.6 0.9 %shard_map.51 = (bf16[256,48]{1,0:T(8,128)(2,1)}, f32[54,8,512]{2,1,0:T(8,128)}) custom-call(bf16[256,48]{1,0:T(8,128)(2,1)S(1)} %get-tuple-element.6.x_ref, f32[54,8,512]{2,1,0:T(8,128)S(1)} %get-tuple-element.7.w_ref), custom_call_target="tpu_custom_call" | custom-call | tf_op jit(solution)/shard_map/pallas_call | solution.py:548

commit v6 on v5

--- a/solution.py
+++ b/solution.py
@@ -217,27 +217,41 @@
     sibling = z * 2 + (1 - core)
     here = {"lat": lat, "lon": lon}
 
+    known = {}
+
+    def z_at(step):
+        if not isinstance(step, int):
+            return lax.rem(z + step + nz, nz) * 2 + core
+        if step not in known:
+            known[step] = lax.rem(z + step + nz, nz) * 2 + core
+        return known[step]
+
+    def side_at(axis, step):
+        step = step % SIDE
+        if step == 0:
+            return here[axis]
+        if (axis, step) not in known:
+            known[axis, step] = lax.rem(here[axis] + step, SIDE)
+        return known[axis, step]
+
+    def plane_at(a, b):
+        return {"lat": side_at("lat", a), "lon": side_at("lon", b)}
+
+    def whole(peer):
+        return peer.get("ch", ch), peer.get("lat", lat), peer.get("lon", lon)
+
+    barrier = pltpu.get_barrier_semaphore()
+    peers = [{"ch": z_at(step)} for step in (4, -4, 3, -3, 2, -2, 1, -1)]
+    peers += [{"ch": sibling}] + [plane_at(a, b) for a, b in OTHERS]
+    for peer in peers:
+        pl.semaphore_signal(barrier, inc=1, device_id=whole(peer), device_id_type=MESH)
+
     fetches = [
         pltpu.make_async_copy(src, dst, in_sem.at[n])
         for n, (src, dst) in enumerate(((g_hbm, g_own), (x_hbm, x_own), (w_hbm, wts)))
     ]
     for fetch in fetches:
         fetch.start()
-
-    def z_at(step):
-        return lax.rem(z + step + nz, nz) * 2 + core
-
-    def side_at(axis, step):
-        return lax.rem(here[axis] + step + SIDE, SIDE)
-
-    def plane_at(a, b):
-        return {"lat": side_at("lat", a), "lon": side_at("lon", b)}
-
-    barrier = pltpu.get_barrier_semaphore()
-    peers = [{"ch": z_at(step)} for step in (4, -4, 3, -3, 2, -2, 1, -1)]
-    peers += [{"ch": sibling}] + [plane_at(a, b) for a, b in OTHERS]
-    for peer in peers:
-        pl.semaphore_signal(barrier, inc=1, device_id=peer, device_id_type=MESH)
 
     places = lane_places(CH)
     spread = spread_matrix()
@@ -255,7 +269,7 @@
             dst_ref=dst,
             send_sem=send_sem,
             recv_sem=recv_sem,
-            device_id=peer,
+            device_id=whole(peer),
             device_id_type=MESH,
         )
 
@@ -284,8 +298,10 @@
         late = 0 if abs(dist) <= 5 else 1
         send(gath.at[slot], gath.at[slot], sib_send, sib_recv.at[late], {"ch": sibling})
 
-    def block_here(dist):
+    def block_here(dist, hops=()):
         arrived(gath.at[z_at(-dist)], z_recv.at[(dist + 7) % 16])
+        for hop in hops:
+            to_chip(dist + hop, hop)
         to_sibling(dist)
 
     for dist in (4, -4, 1, -1):
@@ -308,18 +324,12 @@
             cols[tap * CH : tap * CH + CH, :] = value.astype(BF16)
 
     cols[TAPS * CH :, :] = jnp.zeros((CH, CELLS), BF16)
-    block_here(1)
-    to_chip(2, 1)
-    block_here(-1)
-    to_chip(-2, -1)
+    block_here(1, (1,))
+    block_here(-1, (-1,))
     arrived(field.at[pl.ds(0, 8)], xh_recv)
     build(0)
-    block_here(4)
-    for hop in (3, 1, 2, -1):
-        to_chip(4 + hop, hop)
-    block_here(-4)
-    for hop in (-3, -1, -2, 1):
-        to_chip(-4 + hop, hop)
+    block_here(4, (3, 1, 2, -1))
+    block_here(-4, (-3, -1, -2, 1))
     way = 4 - 8 * core
     far = z_at(-way)
     send(gath.at[far], gath.at[far], z_send, z_recv.at[15], {"ch": z_at(way)})
@@ -331,14 +341,15 @@
         return lax.rem(near_tile + 2 * half + n, 4)
 
     def spread_out(half):
-        largest = None
+        filters = jnp.concatenate(
+            [gath[pl.ds(tile_of(half, n) * 8, 8)].reshape(128, CELLS) for n in range(2)], axis=0
+        )
+        both = lax.dot_general(
+            cols[...], filters, (((1,), (1,)), ((), ())), preferred_element_type=F32
+        )
+        largest = jnp.max(jnp.abs(both), axis=0, keepdims=True)
         for n in range(2):
-            filters = gath[pl.ds(tile_of(half, n) * 8, 8)].reshape(128, CELLS)
-            sums = lax.dot_general(
-                cols[...], filters, (((1,), (1,)), ((), ())), preferred_element_type=F32
-            )
-            most = jnp.max(jnp.abs(sums), axis=0, keepdims=True)
-            largest = most if largest is None else jnp.maximum(largest, most)
+            sums = both[:, n * 128 : n * 128 + 128]
             for a in range(SIDE):
                 for side in range(2):
                     at = (2 * a + side) * PART

time: 42.6 us -> 42.6 us (level)
  no operation moved by 1% of the time
where the time goes in v6:
time: 42.6 us; the launch traced here: 42.5 us
  Pallas kernels  41.9 us (98%)
  between operations  0.64 us (2%)
    pallas_call x1, Pallas kernels, body(): pl.pallas_call(lambda *refs: kernel(nz, 1.0 / math.sqrt(cells), *refs), o...  40.9 us
    pallas_call x1, Pallas kernels, body(): pl.pallas_call(keep_both, out_shape=(jax.ShapeDtypeStruct((CH * GROUPS, C...  0.94 us

profile of v6, /device:TPU:1, one launch (start us, length us, event | category | flops | bytes accessed | tf_op | source)
XLA Modules:
  0.0 42.5 jit_solution(5676415700218660702)
XLA Ops:
  0.6 40.9 %shard_map.50 = (bf16[256,48]{1,0:T(8,128)(2,1)S(1)}, f32[54,8,512]{2,1,0:T(8,128)S(1)}) custom-call(bf16[256,48]{1,0:T(8,128)(2,1)} %bitcast.8, bf16[27,16,512]{2,1,0:T(8,128)(2,1)} %bitcast.7, bf16[256,48]{1,0:T(8,128)(2,1)} %bitcast.9), custom_call_target="tpu_custom_call" | custom-call | tf_op jit(solution)/shard_map/pallas_call | solution.py:506
  41.6 0.9 %shard_map.51 = (bf16[256,48]{1,0:T(8,128)(2,1)}, f32[54,8,512]{2,1,0:T(8,128)}) custom-call(bf16[256,48]{1,0:T(8,128)(2,1)S(1)} %get-tuple-element.6.x_ref, f32[54,8,512]{2,1,0:T(8,128)S(1)} %get-tuple-element.7.w_ref), custom_call_target="tpu_custom_call" | custom-call | tf_op jit(solution)/shard_map/pallas_call | solution.py:559

commit v7 on v6

--- a/solution.py
+++ b/solution.py
@@ -26,10 +26,7 @@
 TOP = 2.0**30
 TINY = 1e-28
 VMEM_BYTES = 24 << 20
-OTHERS = sorted(
-    ((a, b) for a in range(SIDE) for b in range(SIDE) if (a, b) != (0, 0)),
-    key=lambda at: -(min(at[0], SIDE - at[0]) + min(at[1], SIDE - at[1])),
-)
+OTHERS = [(2, 2), (1, 2), (2, 3), (3, 2), (2, 1), (1, 1), (3, 3), (1, 3), (3, 1), (0, 2), (2, 0), (0, 1), (1, 0), (0, 3), (3, 0)]
 PIECES = (((0, PART + 8),), ((0, PART + 8),))
 ORDER = [(half, piece) for half in range(2) for piece in range(len(PIECES[half]))]
 NEAR = [(a, b) for a in (-1, 0, 1) for b in (-1, 0, 1) if (a, b) != (0, 0)]

time: 42.6 us -> 42.5 us (level)
  no operation moved by 1% of the time
where the time goes in v7:
time: 42.5 us; the launch traced here: 42.3 us
  Pallas kernels  41.7 us (98%)
  between operations  0.64 us (2%)
    pallas_call x1, Pallas kernels, body(): pl.pallas_call(lambda *refs: kernel(nz, 1.0 / math.sqrt(cells), *refs), o...  40.7 us
    pallas_call x1, Pallas kernels, body(): pl.pallas_call(keep_both, out_shape=(jax.ShapeDtypeStruct((CH * GROUPS, C...  0.94 us

profile of v7, /device:TPU:1, one launch (start us, length us, event | category | flops | bytes accessed | tf_op | source)
XLA Modules:
  0.0 42.3 jit_solution(6452393978533419897)
XLA Ops:
  0.6 40.7 %shard_map.50 = (bf16[256,48]{1,0:T(8,128)(2,1)S(1)}, f32[54,8,512]{2,1,0:T(8,128)S(1)}) custom-call(bf16[256,48]{1,0:T(8,128)(2,1)} %bitcast.8, bf16[27,16,512]{2,1,0:T(8,128)(2,1)} %bitcast.7, bf16[256,48]{1,0:T(8,128)(2,1)} %bitcast.9), custom_call_target="tpu_custom_call" | custom-call | tf_op jit(solution)/shard_map/pallas_call | solution.py:503
  41.4 0.9 %shard_map.51 = (bf16[256,48]{1,0:T(8,128)(2,1)}, f32[54,8,512]{2,1,0:T(8,128)}) custom-call(bf16[256,48]{1,0:T(8,128)(2,1)S(1)} %get-tuple-element.6.x_ref, f32[54,8,512]{2,1,0:T(8,128)S(1)} %get-tuple-element.7.w_ref), custom_call_target="tpu_custom_call" | custom-call | tf_op jit(solution)/shard_map/pallas_call | solution.py:556
